TPU v7x, 32 devices: a whole 2x2x4 slice. The times are simulated.
32 devices in a mesh: gx: 8 (over z, core), gy: 4 (over y, x).
Axes of the slice: x: 2, y: 2, z: 4, core: 2. Of those that a mesh axis runs over, the one named last changes fastest.
Arguments:
- grad_pressure: float32 [64, 128, 1024], P('gx', 'gy'), may hold values from -6 to 6
- beta: float32 [3, 64, 128, 1024], P(None, 'gx', 'gy'), may hold values from 0.25 to 4
- tile_rows: int32 [8192], P(('gx', 'gy')), may hold values from 0 to 2047
- tile_owner: int32 [8192, 1], P(('gx', 'gy')), may hold values from 0 to 31; in each aligned block of 256 rows (0 to 255, 256 to 511, ...) at most 8 rows name the same one
- tile_slot: int32 [8192], P(('gx', 'gy')), may hold values from 0 to 255
- face_mask: int32 [8192, 128], P(('gx', 'gy')), may hold values 0 or 1
- heights: float32 [3, 8192, 128], P(None, ('gx', 'gy')), may hold values from -6 to 6
Outputs:
- grad_rhs: float32 [64, 128, 1024], P('gx', 'gy')
- grad_heights: float32 [3, 8192, 128], P(None, ('gx', 'gy'))
Inputs may be any that keep to these rules, and one draw needn't show every extreme that they name: `tile_rows`: each entry indexes a row of 128 cells inside its own device's block. `tile_owner`: among the 256 tiles of one device no owner is named more than 8 times.
All inputs are finite; a program needn't handle non-finite values. No bound on the sum of `face_mask` on one device may be relied on, other than what follows from the above.
Results may differ from a plain program's by a relative error of at most 0.000025.
Values sent between devices are 32-bit elements; how exact they have to be, the bound alone decides.
A program may use at most 192 MiB of HBM per device.

v0:
```python
import functools
import math

import jax
import jax.numpy as jnp
from jax import lax
from jax.experimental import pallas as pl
from jax.experimental.pallas import tpu as pltpu
from jax.sharding import PartitionSpec as P

ITERS = 3
STEPS = 4
CAP = 8
LANES = 128
ROWS = 8

LOW_BOUND = 0.1
HIGH_BOUND = 1.9

MESH = pl.DeviceIdType.MESH
EXACT = lax.Precision.HIGHEST


def omega_of(step_index):
    theta = 0.5 * (HIGH_BOUND + LOW_BOUND) + 0.5 * (HIGH_BOUND - LOW_BOUND) * math.cos(
        math.pi * (2 * step_index + 1) / (2 * STEPS)
    )
    return 1.0 / theta


def omega_at(step):
    j = STEPS - 1 - step % STEPS
    value = jnp.float32(omega_of(0))
    for index in range(1, STEPS):
        value = jnp.where(j == index, jnp.float32(omega_of(index)), value)
    return value


def picked_sum(selector, rows):
    high = rows.astype(jnp.bfloat16)
    rest = rows - high.astype(jnp.float32)
    middle = rest.astype(jnp.bfloat16)
    low = (rest - middle.astype(jnp.float32)).astype(jnp.bfloat16)
    parts = [jnp.dot(selector, part, preferred_element_type=jnp.float32) for part in (high, middle, low)]
    return parts[0] + (parts[1] + parts[2])


def kernel(
    n_x, n_y,
    grad_in, beta_in, rows_in, owner_in, slot_in, mask_in, heights_in,
    out_hbm, back_ref,
    out_ref,
    grad_ref, beta_ref, rows_ref, owner_ref, slot_ref, mask_ref, heights_ref, load_sem,
    coeff, state, halo_x, halo_y, face_y, rim_x, rim_y, rim_face, face_coeff,
    flat, picked, place, send_rows, recv_rows, send_slots, recv_slots,
    rim_send, rim_recv, x_send, x_recv, y_send, y_recv, row_send, row_recv, slot_send, slot_recv,
):
    X, Y, Z = grad_ref.shape
    groups = Y // ROWS
    blocks = Z // LANES
    tiles = rows_ref.shape[0]
    peers = n_x * n_y
    slots = heights_ref.shape[1]
    ix = lax.axis_index("gx")
    iy = lax.axis_index("gy")
    me = ix * n_y + iy
    has_x = (ix > 0, ix < n_x - 1)
    has_y = (iy > 0, iy < n_y - 1)
    at_x = ((ix - 1, iy), (ix + 1, iy))
    at_y = ((ix, iy - 1), (ix, iy + 1))

    rim_x[...] = jnp.zeros_like(rim_x)
    rim_y[...] = jnp.zeros_like(rim_y)
    halo_x[...] = jnp.zeros_like(halo_x)
    halo_y[...] = jnp.zeros_like(halo_y)

    def peer_at(step):
        peer = (me + step) % peers
        return peer, (peer // n_y, peer % n_y)

    barrier = pltpu.get_barrier_semaphore()

    @pl.loop(1, peers)
    def _(step):
        pl.semaphore_signal(barrier, inc=1, device_id=peer_at(step)[1], device_id_type=MESH)

    names = ("owner", "slot", "beta", "grad", "rows", "mask", "heights")
    pairs = (
        (owner_in, owner_ref), (slot_in, slot_ref), (beta_in, beta_ref), (grad_in, grad_ref),
        (rows_in, rows_ref), (mask_in, mask_ref), (heights_in, heights_ref),
    )
    loads = {
        name: pltpu.make_async_copy(source, held, load_sem.at[index])
        for index, (name, (source, held)) in enumerate(zip(names, pairs))
    }
    for name in names:
        loads[name].start()
    for name in ("owner", "slot"):
        loads[name].wait()

    owner = owner_ref[...]
    peer_ids = lax.broadcasted_iota(jnp.int32, (peers, tiles), 0)
    named = (owner == peer_ids).astype(jnp.float32)
    down = lax.broadcasted_iota(jnp.int32, (tiles, tiles), 0)
    across = lax.broadcasted_iota(jnp.int32, (tiles, tiles), 1)
    earlier = (down < across).astype(jnp.bfloat16)
    counts = jnp.dot(named.astype(jnp.bfloat16), earlier, preferred_element_type=jnp.float32)
    position = jnp.sum(counts * named, axis=0, keepdims=True)
    target = owner.astype(jnp.float32) * CAP + position
    spots = lax.broadcasted_iota(jnp.int32, (peers * CAP, tiles), 0).astype(jnp.float32)
    place[...] = (target == spots).astype(jnp.float32).astype(jnp.bfloat16)
    spread = lax.broadcasted_iota(jnp.int32, (LANES, tiles), 0).astype(jnp.float32)
    spread = (spread == position).astype(jnp.float32)
    slot_rows = lax.dot_general(
        named * slot_ref[...].astype(jnp.float32), spread, (((1,), (1,)), ((), ())),
        preferred_element_type=jnp.float32, precision=EXACT,
    )
    send_slots[...] = slot_rows.reshape(peers, 1, LANES)

    loads["beta"].wait()
    for x in range(X):
        rim_face[x : x + 1, :] = beta_ref[1, x, Y - 1 : Y, :]

    pl.semaphore_wait(barrier, peers - 1)

    def rim_copies():
        return (
            (has_x, pltpu.make_async_remote_copy(
                beta_ref.at[0, X - 1], rim_x, rim_send.at[0], rim_recv.at[0],
                device_id=at_x[1], device_id_type=MESH)),
            (has_y, pltpu.make_async_remote_copy(
                rim_face, rim_y, rim_send.at[1], rim_recv.at[1],
                device_id=at_y[1], device_id_type=MESH)),
        )

    for has, copy in rim_copies():
        @pl.when(has[1])
        def _():
            copy.start()

    def slot_copy(step):
        peer, place_of = peer_at(step)
        return pltpu.make_async_remote_copy(
            send_slots.at[peer], recv_slots.at[me], slot_send.at[peer], slot_recv.at[me],
            device_id=place_of, device_id_type=MESH)

    def row_copy(step):
        peer, place_of = peer_at(step)
        return pltpu.make_async_remote_copy(
            send_rows.at[peer], recv_rows.at[me], row_send.at[peer], row_recv.at[me],
            device_id=place_of, device_id_type=MESH)

    def rows_of(g):
        return pl.ds(g * ROWS, ROWS)

    def x_copy(par, side, g):
        return pltpu.make_async_remote_copy(
            state.at[par, (X - 1) * side, rows_of(g)], halo_x.at[par, 1 - side, rows_of(g)],
            x_send.at[par, side, g], x_recv.at[par, 1 - side, g],
            device_id=at_x[side], device_id_type=MESH)

    def y_copy(par, side):
        return pltpu.make_async_remote_copy(
            face_y.at[par, side], halo_y.at[par, 1 - side],
            y_send.at[par, side], y_recv.at[par, 1 - side],
            device_id=at_y[side], device_id_type=MESH)

    def x_arrival(par, side, g):
        return pltpu.make_async_remote_copy(
            state.at[par, 0, rows_of(g)], halo_x.at[par, side, rows_of(g)],
            x_send.at[par, side, g], x_recv.at[par, side, g],
            device_id=at_x[side], device_id_type=MESH)

    def y_arrival(par, side):
        return pltpu.make_async_remote_copy(
            face_y.at[par, side], halo_y.at[par, side],
            y_send.at[par, side], y_recv.at[par, side],
            device_id=at_y[side], device_id_type=MESH)

    row_ids = lax.broadcasted_iota(jnp.int32, (ROWS, Z), 0)
    z_ids = lax.broadcasted_iota(jnp.int32, (ROWS, Z), 1)

    def from_below(tile, row):
        return jnp.where(row_ids == 0, row, pltpu.roll(tile, 1, 0))

    def from_above(tile, row):
        return jnp.where(row_ids == ROWS - 1, row, pltpu.roll(tile, ROWS - 1, 0))

    def prepare(x, g):
        r = slice(g * ROWS, (g + 1) * ROWS)
        up_x, up_y, up_z = beta_ref[0, x, r, :], beta_ref[1, x, r, :], beta_ref[2, x, r, :]
        low_x = rim_x[r, :] if x == 0 else beta_ref[0, x - 1, r, :]
        row = rim_y[x : x + 1, :] if g == 0 else beta_ref[1, x, g * ROWS - 1 : g * ROWS, :]
        low_y = from_below(up_y, row)
        low_z = jnp.where(z_ids == 0, 0.0, pltpu.roll(up_z, 1, 1))
        inv = 1.0 / (up_x + low_x + up_y + low_y + up_z + low_z)
        up_z = jnp.where(z_ids == Z - 1, 0.0, up_z)
        for index, value in enumerate((up_x, low_x, up_y, low_y, up_z, low_z)):
            value = value * inv
            coeff[index, x, r, :] = value
            if index == 3 and g == 0:
                face_coeff[0, x : x + 1, :] = value[:1, :]
            if index == 2 and g == groups - 1:
                face_coeff[1, x : x + 1, :] = value[ROWS - 1 :, :]
        value = inv * grad_ref[x, r, :]
        state[0, x, r, :] = value
        out_ref[x, r, :] = jnp.zeros_like(value)
        if g == 0:
            face_y[0, 0, x : x + 1, :] = value[:1, :]
        if g == groups - 1:
            face_y[0, 1, x : x + 1, :] = value[ROWS - 1 :, :]

    loads["grad"].wait()
    for x in range(1, X):
        for g in range(1, groups):
            prepare(x, g)
    (_, rim_x_copy), (_, rim_y_copy) = rim_copies()

    @pl.when(has_x[0])
    def _():
        rim_x_copy.wait_recv()

    for g in range(1, groups):
        prepare(0, g)
        for side in range(2):
            @pl.when(has_x[side])
            def _():
                x_copy(0, side, g).start()

    @pl.when(has_y[0])
    def _():
        rim_y_copy.wait_recv()

    @pl.when(has_y[1])
    def _():
        y_copy(0, 1).start()

    prepare(0, 0)
    prepare(X - 1, 0)
    for side in range(2):
        @pl.when(has_x[side])
        def _():
            x_copy(0, side, 0).start()
    for x in range(1, X - 1):
        prepare(x, 0)

    @pl.when(has_y[0])
    def _():
        y_copy(0, 0).start()

    for has, copy in rim_copies():
        @pl.when(has[1])
        def _():
            copy.wait_send()

    @pl.loop(1, peers)
    def _(step):
        slot_copy(step).start()

    recv_slots[me] = send_slots[me]

    total = ITERS * STEPS

    def faces_of(par, value, x, g):
        if g == 0:
            face_y[par, 0, x : x + 1, :] = value[:1, :]
        if g == groups - 1:
            face_y[par, 1, x : x + 1, :] = value[ROWS - 1 :, :]

    def update(par, omega, x, g):
        r = slice(g * ROWS, (g + 1) * ROWS)
        s = state[par, x, r, :]
        out_ref[x, r, :] += omega * s
        if g == groups - 1:
            above_row = 0.0
        else:
            above_row = state[par, x, (g + 1) * ROWS : (g + 1) * ROWS + 1, :]
        if g == 0:
            below_row = 0.0
        else:
            below_row = state[par, x, g * ROWS - 1 : g * ROWS, :]
        beside = coeff[2, x, r, :] * from_above(s, above_row)
        beside += coeff[3, x, r, :] * from_below(s, below_row)
        beside += coeff[4, x, r, :] * pltpu.roll(s, Z - 1, 1)
        beside += coeff[5, x, r, :] * pltpu.roll(s, 1, 1)
        if x < X - 1:
            beside += coeff[0, x, r, :] * state[par, x + 1, r, :]
        if x > 0:
            beside += coeff[1, x, r, :] * state[par, x - 1, r, :]
        value = s + omega * (beside - s)
        state[1 - par, x, r, :] = value
        if 0 < x < X - 1:
            faces_of(1 - par, value, x, g)

    def add_halo_x(par, omega, side, g):
        @pl.when(has_x[side])
        def _():
            x_arrival(par, side, g).wait_recv()

        x = (X - 1) * side
        r = slice(g * ROWS, (g + 1) * ROWS)
        value = state[1 - par, x, r, :] + omega * (coeff[1 - side, x, r, :] * halo_x[par, side, r, :])
        state[1 - par, x, r, :] = value
        faces_of(1 - par, value, x, g)

    def finish_sends(par, go):
        for side in range(2):
            for g in range(groups):
                @pl.when(jnp.logical_and(has_x[side], go))
                def _():
                    x_copy(par, side, g).wait_send()

            @pl.when(jnp.logical_and(has_y[side], go))
            def _():
                y_copy(par, side).wait_send()

    def step_body(step, carry):
        par = step % 2
        omega = omega_at(step)
        more = step + 2 < total
        finish_sends(1 - par, step > 0)
        for x in range(X):
            for g in range(groups):
                update(par, omega, x, g)

        def send_x(side, g):
            @pl.when(jnp.logical_and(has_x[side], more))
            def _():
                x_copy(1 - par, side, g).start()

        for g in range(1, groups - 1):
            for side in range(2):
                add_halo_x(par, omega, side, g)
                send_x(side, g)
        ends = (0, groups - 1)
        for g in ends:
            for side in range(2):
                add_halo_x(par, omega, side, g)
        for side in range(2):
            @pl.when(has_y[side])
            def _():
                y_arrival(par, side).wait_recv()

            face = face_y[1 - par, side] + omega * (face_coeff[side] * halo_y[par, side])
            face_y[1 - par, side] = face

            @pl.when(jnp.logical_and(has_y[side], more))
            def _():
                y_copy(1 - par, side).start()

            row = (Y - 1) * side
            for x in range(X):
                state[1 - par, x, row : row + 1, :] = face[x : x + 1, :]
            for x_side in range(2):
                send_x(x_side, ends[side])
        return carry

    lax.fori_loop(0, total - 1, step_body, 0)
    finish_sends((total - 2) % 2, True)
    for name in ("rows", "mask", "heights"):
        loads[name].wait()

    last = omega_of(STEPS - 1 - (total - 1) % STEPS)

    for x in range(X):
        for b in range(blocks):
            start = (x * blocks + b) * Y
            cut = slice(b * LANES, (b + 1) * LANES)
            value = out_ref[x, :, cut] + last * state[(total - 1) % 2, x, :, cut]
            out_ref[x, :, cut] = value
            flat[start : start + Y, :] = value

    store = pltpu.make_async_copy(out_ref, out_hbm, load_sem.at[7])
    store.start()
    unroll = 8

    @pl.loop(0, tiles // unroll)
    def _(chunk):
        for lane in range(unroll):
            t = chunk * unroll + lane
            row = rows_ref[t]
            line = lax.div(row, blocks)
            x = lax.div(line, Y)
            at = (x * blocks + row - line * blocks) * Y + line - x * Y
            picked[pl.ds(t, 1), :] = flat[pl.ds(at, 1), :]

    jumps = picked[...] * mask_ref[...].astype(jnp.float32)
    send_rows[...] = picked_sum(place[...], jumps).reshape(peers, CAP, LANES)

    @pl.loop(1, peers)
    def _(step):
        row_copy(step).start()

    recv_rows[me] = send_rows[me]

    @pl.loop(1, peers)
    def _(step):
        peer, place_of = peer_at(step)
        pltpu.make_async_remote_copy(
            send_slots.at[peer], recv_slots.at[peer], slot_send.at[peer], slot_recv.at[peer],
            device_id=place_of, device_id_type=MESH).wait()

    own = lax.broadcasted_iota(jnp.int32, (peers, CAP, LANES), 1)
    lane_ids = lax.broadcasted_iota(jnp.int32, (peers, CAP, LANES), 2)
    got = jnp.broadcast_to(recv_slots[...], (peers, CAP, LANES))
    slot_of = jnp.sum(jnp.where(own == lane_ids, got, 0.0), axis=2, keepdims=True)
    slot_of = slot_of.reshape(peers * CAP, 1)
    slot_ids = lax.broadcasted_iota(jnp.int32, (peers * CAP, slots), 1).astype(jnp.float32)
    chosen = (slot_of == slot_ids).astype(jnp.float32).T.astype(jnp.bfloat16)

    slope = 0.5 * (heights_ref[2] - heights_ref[0])
    bend = heights_ref[2] - 2.0 * heights_ref[1] + heights_ref[0]
    denom = 1.0 + slope * slope
    factor = 1.0 / (denom * jnp.sqrt(denom))
    skew = -3.0 * slope * bend * factor / denom

    @pl.loop(1, peers)
    def _(step):
        peer, place_of = peer_at(step)
        pltpu.make_async_remote_copy(
            send_rows.at[peer], recv_rows.at[peer], row_send.at[peer], row_recv.at[peer],
            device_id=place_of, device_id_type=MESH).wait()

    table = picked_sum(chosen, recv_rows[...].reshape(peers * CAP, LANES))
    back_ref[0] = table * (factor - 0.5 * skew)
    back_ref[1] = -2.0 * table * factor
    back_ref[2] = table * (factor + 0.5 * skew)
    store.wait()


def shards(grad_pressure, beta, tile_rows, tile_owner, tile_slot, face_mask, heights):
    n_x, n_y = lax.axis_size("gx"), lax.axis_size("gy")
    peers = n_x * n_y
    X, Y, Z = grad_pressure.shape
    groups = Y // ROWS
    tiles = tile_rows.shape[0]
    f32 = jnp.float32
    vmem = pl.BlockSpec(memory_space=pltpu.VMEM)
    hbm = pl.BlockSpec(memory_space=pltpu.HBM)
    dma = pltpu.SemaphoreType.DMA
    return pl.pallas_call(
        functools.partial(kernel, n_x, n_y),
        out_shape=(
            jax.ShapeDtypeStruct((X, Y, Z), f32),
            jax.ShapeDtypeStruct(heights.shape, f32),
        ),
        in_specs=[hbm] * 7,
        out_specs=(hbm, vmem),
        scratch_shapes=[
            pltpu.VMEM((X, Y, Z), f32),
            pltpu.VMEM((X, Y, Z), f32),
            pltpu.VMEM(beta.shape, f32),
            pltpu.SMEM((tiles,), jnp.int32),
            pltpu.VMEM((1, tiles), jnp.int32),
            pltpu.VMEM((1, tiles), jnp.int32),
            pltpu.VMEM(face_mask.shape, jnp.int32),
            pltpu.VMEM(heights.shape, f32),
            dma((8,)),
            pltpu.VMEM((6, X, Y, Z), f32),
            pltpu.VMEM((2, X, Y, Z), f32),
            pltpu.VMEM((2, 2, Y, Z), f32),
            pltpu.VMEM((2, 2, X, Z), f32),
            pltpu.VMEM((2, 2, X, Z), f32),
            pltpu.VMEM((Y, Z), f32),
            pltpu.VMEM((X, Z), f32),
            pltpu.VMEM((X, Z), f32),
            pltpu.VMEM((2, X, Z), f32),
            pltpu.VMEM((X * Y * Z // LANES, LANES), f32),
            pltpu.VMEM((tiles, LANES), f32),
            pltpu.VMEM((peers * CAP, tiles), jnp.bfloat16),
            pltpu.VMEM((peers, CAP, LANES), f32),
            pltpu.VMEM((peers, CAP, LANES), f32),
            pltpu.VMEM((peers, 1, LANES), f32),
            pltpu.VMEM((peers, 1, LANES), f32),
            dma((2,)),
            dma((2,)),
            dma((2, 2, groups)),
            dma((2, 2, groups)),
            dma((2, 2)),
            dma((2, 2)),
            dma((peers,)),
            dma((peers,)),
            dma((peers,)),
            dma((peers,)),
        ],
        compiler_params=pltpu.CompilerParams(
            collective_id=0, has_side_effects=True, vmem_limit_bytes=56 * 1024 * 1024
        ),
    )(grad_pressure, beta, tile_rows, tile_owner.reshape(1, -1), tile_slot.reshape(1, -1), face_mask, heights)


def solution(mesh):
    in_specs = (
        P("gx", "gy", None),
        P(None, "gx", "gy", None),
        P(("gx", "gy")),
        P(("gx", "gy"), None),
        P(("gx", "gy")),
        P(("gx", "gy"), None),
        P(None, ("gx", "gy"), None),
    )
    out_specs = (P("gx", "gy", None), P(None, ("gx", "gy"), None))
    return jax.shard_map(shards, mesh=mesh, in_specs=in_specs, out_specs=out_specs, check_vma=False)
```

profile of v0, /device:TPU:0, one launch (start us, length us, event | category | flops | bytes accessed | tf_op | source)
XLA Modules:
  0.0 62.1 jit_solution(9641379106603574635)
XLA Ops:
  0.6 57.4 %shard_map.86 = (f32[8,32,1024]{2,1,0:T(8,128)}, f32[3,256,128]{2,1,0:T(8,128)}) custom-call(f32[8,32,1024]{2,1,0:T(8,128)} %grad_in.1, f32[3,8,32,1024]{3,2,1,0:T(8,128)} %beta_in.1, s32[256]{0:T(256)} %rows_in.1, s32[1,256]{1,0:T(1,128)} %bitcast.2, s32[1,256]{1,0:T(1,128)} %bitcast.3, s32[256,128]{1,0:T(8,128)} %mask_in.1, f32[3,256,128]{2,1,0:T(8,128)} %heights_in.1), custom_call_target="tpu_custom_call" | custom-call | tf_op jit(solution)/shard_map/pallas_call | solution.py:441
  58.1 2.3 %copy.11 = f32[8,32,1024]{2,1,0:T(8,128)} copy(f32[8,32,1024]{2,1,0:T(8,128)} %get-tuple-element.4) | data formatting | bytes 2097152
  60.4 1.8 %copy.12 = f32[3,256,128]{2,1,0:T(8,128)} copy(f32[3,256,128]{2,1,0:T(8,128)} %get-tuple-element.5) | data formatting | bytes 786432
where the time goes:
time: 62.3 us; the launch traced here: 62.1 us
  Pallas kernels  57.4 us (92%)
  local copies, waits for them, and re-layouts  4.07 us (7%)
  between operations  0.64 us (1%)
    pallas_call x1, Pallas kernels, shards(): pl.pallas_call(functools.partial(kernel, n_x, n_y), out_shape=(jax.ShapeD...  57.4 us
    unnamed x2, local copies, waits for them, and re-layouts  4.07 us

commit v1 on v0

v1 whole, which is shorter than its diff:
```python
import functools
import math

import jax
import jax.numpy as jnp
from jax import lax
from jax.experimental import pallas as pl
from jax.experimental.pallas import tpu as pltpu
from jax.sharding import PartitionSpec as P

ITERS = 3
STEPS = 4
CAP = 8
LANES = 128
ROWS = 8
WIDE = 256

LOW_BOUND = 0.1
HIGH_BOUND = 1.9

MESH = pl.DeviceIdType.MESH
EXACT = lax.Precision.HIGHEST


def omega_of(step_index):
    theta = 0.5 * (HIGH_BOUND + LOW_BOUND) + 0.5 * (HIGH_BOUND - LOW_BOUND) * math.cos(
        math.pi * (2 * step_index + 1) / (2 * STEPS)
    )
    return 1.0 / theta


def omega_at(step):
    j = STEPS - 1 - step % STEPS
    value = jnp.float32(omega_of(0))
    for index in range(1, STEPS):
        value = jnp.where(j == index, jnp.float32(omega_of(index)), value)
    return value


def picked_sum(selector, rows):
    high = rows.astype(jnp.bfloat16)
    rest = rows - high.astype(jnp.float32)
    middle = rest.astype(jnp.bfloat16)
    low = (rest - middle.astype(jnp.float32)).astype(jnp.bfloat16)
    parts = [jnp.dot(selector, part, preferred_element_type=jnp.float32) for part in (high, middle, low)]
    return parts[0] + (parts[1] + parts[2])


def kernel(
    n_x, n_y,
    grad_in, beta_in, rows_in, owner_in, slot_in, mask_in, heights_in,
    out_hbm, back_ref,
    grad_ref, beta_ref, rows_ref, owner_ref, slot_ref, mask_ref, heights_ref, load_sem,
    coeff, target, state, face_y, corner, halo_x, halo_y, halo_d,
    rim_x, rim_y, rim_face, face_coeff, edge_x, edge_y, near_x, near_y, line_x, line_y,
    flat, picked, place, send_rows, recv_rows, send_slots, recv_slots,
    rim_send, rim_recv, x_send, x_recv, y_send, y_recv, d_send, d_recv,
    edge_send, edge_recv, side_send, side_recv, row_send, row_recv, slot_send, slot_recv,
):
    X, Y, Z = grad_ref.shape
    groups = Y // ROWS
    blocks = Z // LANES
    chunks = Z // WIDE
    tiles = rows_ref.shape[0]
    peers = n_x * n_y
    slots = heights_ref.shape[1]
    ix = lax.axis_index("gx")
    iy = lax.axis_index("gy")
    me = ix * n_y + iy
    has_x = (ix > 0, ix < n_x - 1)
    has_y = (iy > 0, iy < n_y - 1)
    at_x = ((ix - 1, iy), (ix + 1, iy))
    at_y = ((ix, iy - 1), (ix, iy + 1))
    sides = (0, 1)
    total = ITERS * STEPS
    rounds = (total - 2) // 2

    for ref in (rim_x, rim_y, halo_x, halo_y, halo_d, edge_x, edge_y, line_x, line_y):
        ref[...] = jnp.zeros_like(ref)

    def peer_at(step):
        peer = (me + step) % peers
        return peer, (peer // n_y, peer % n_y)

    barrier = pltpu.get_barrier_semaphore()

    @pl.loop(1, peers)
    def _(step):
        pl.semaphore_signal(barrier, inc=1, device_id=peer_at(step)[1], device_id_type=MESH)

    names = ("owner", "slot", "beta", "grad", "rows", "mask", "heights")
    pairs = (
        (owner_in, owner_ref), (slot_in, slot_ref), (beta_in, beta_ref), (grad_in, grad_ref),
        (rows_in, rows_ref), (mask_in, mask_ref), (heights_in, heights_ref),
    )
    loads = {
        name: pltpu.make_async_copy(source, held, load_sem.at[index])
        for index, (name, (source, held)) in enumerate(zip(names, pairs))
    }
    for name in names:
        loads[name].start()
    for name in ("owner", "slot"):
        loads[name].wait()

    owner = owner_ref[...]
    peer_ids = lax.broadcasted_iota(jnp.int32, (peers, tiles), 0)
    named = (owner == peer_ids).astype(jnp.float32)
    down = lax.broadcasted_iota(jnp.int32, (tiles, tiles), 0)
    across = lax.broadcasted_iota(jnp.int32, (tiles, tiles), 1)
    earlier = (down < across).astype(jnp.bfloat16)
    counts = jnp.dot(named.astype(jnp.bfloat16), earlier, preferred_element_type=jnp.float32)
    position = jnp.sum(counts * named, axis=0, keepdims=True)
    spot = owner.astype(jnp.float32) * CAP + position
    spots = lax.broadcasted_iota(jnp.int32, (peers * CAP, tiles), 0).astype(jnp.float32)
    place[...] = (spot == spots).astype(jnp.float32).astype(jnp.bfloat16)
    spread = lax.broadcasted_iota(jnp.int32, (LANES, tiles), 0).astype(jnp.float32)
    spread = (spread == position).astype(jnp.float32)
    slot_rows = lax.dot_general(
        named * slot_ref[...].astype(jnp.float32), spread, (((1,), (1,)), ((), ())),
        preferred_element_type=jnp.float32, precision=EXACT,
    )
    send_slots[...] = slot_rows.reshape(peers, 1, LANES)

    loads["beta"].wait()
    for x in range(X):
        rim_face[x : x + 1, :] = beta_ref[1, x, Y - 1 : Y, :]

    pl.semaphore_wait(barrier, peers - 1)

    def remote(source, landing, send, recv, place_of):
        return pltpu.make_async_remote_copy(source, landing, send, recv, device_id=place_of, device_id_type=MESH)

    def rim_copies():
        return (
            (has_x, remote(beta_ref.at[0, X - 1], rim_x, rim_send.at[0], rim_recv.at[0], at_x[1])),
            (has_y, remote(rim_face, rim_y, rim_send.at[1], rim_recv.at[1], at_y[1])),
        )

    for has, copy in rim_copies():
        @pl.when(has[1])
        def _():
            copy.start()

    def slot_copy(step):
        peer, place_of = peer_at(step)
        return pltpu.make_async_remote_copy(
            send_slots.at[peer], recv_slots.at[me], slot_send.at[peer], slot_recv.at[me],
            device_id=place_of, device_id_type=MESH)

    def row_copy(step):
        peer, place_of = peer_at(step)
        return pltpu.make_async_remote_copy(
            send_rows.at[peer], recv_rows.at[me], row_send.at[peer], row_recv.at[me],
            device_id=place_of, device_id_type=MESH)

    def lanes(q):
        return pl.ds(q * WIDE, WIDE)

    def x_copy(par, kind, side, q, land):
        return remote(
            state.at[kind, (X - 1) * side, :, lanes(q)], halo_x.at[par, kind, land, :, lanes(q)],
            x_send.at[kind, side, q], x_recv.at[par, kind, land, q], at_x[side])

    def y_copy(par, kind, side, q, land):
        return remote(
            face_y.at[kind, side, :, lanes(q)], halo_y.at[par, kind, land, :, lanes(q)],
            y_send.at[kind, side, q], y_recv.at[par, kind, land, q], at_y[side])

    def d_copy(par, dx, dy, q, land):
        return remote(
            corner.at[dx, dy, :, lanes(q)], halo_d.at[par, land[0], land[1], :, lanes(q)],
            d_send.at[dx, dy, q], d_recv.at[par, land[0], land[1], q], (at_x[dx][0], at_y[dy][1]))

    def copies_of(par, kind, q, arriving):
        found = []
        for side in sides:
            land = side if arriving else 1 - side
            found.append((has_x[side], x_copy(par, kind, side, q, land)))
        for side in sides:
            land = side if arriving else 1 - side
            found.append((has_y[side], y_copy(par, kind, side, q, land)))
        if kind == 0:
            for dx in sides:
                for dy in sides:
                    land = (dx, dy) if arriving else (1 - dx, 1 - dy)
                    found.append((jnp.logical_and(has_x[dx], has_y[dy]), d_copy(par, dx, dy, q, land)))
        return found

    def start_sends(par, kind, q, go=None):
        for has, copy in copies_of(par, kind, q, False):
            @pl.when(has if go is None else jnp.logical_and(has, go))
            def _():
                copy.start()

    def wait_sends(kind, q):
        for has, copy in copies_of(0, kind, q, False):
            @pl.when(has)
            def _():
                copy.wait_send()

    def wait_arrivals(par, kind, q):
        for has, copy in copies_of(par, kind, q, True):
            @pl.when(has)
            def _():
                copy.wait_recv()

    def edge_copy(side, q, land):
        return remote(
            coeff.at[1 - side, (X - 1) * side, :, lanes(q)], edge_x.at[land, :, lanes(q)],
            edge_send.at[side, q], edge_recv.at[land, q], at_x[side])

    def side_copies(side, land):
        return (
            (has_y[side], remote(face_coeff.at[side], edge_y.at[land], side_send.at[0, side], side_recv.at[0, land], at_y[side])),
            (has_x[side], remote(near_x.at[side], line_x.at[land], side_send.at[1, side], side_recv.at[1, land], at_x[side])),
            (has_y[side], remote(near_y.at[side], line_y.at[land], side_send.at[2, side], side_recv.at[2, land], at_y[side])),
        )

    def row_index(width):
        return lax.broadcasted_iota(jnp.int32, (ROWS, width), 0)

    z_ids = lax.broadcasted_iota(jnp.int32, (ROWS, Z), 1)

    def from_below(tile, row):
        return jnp.where(row_index(tile.shape[1]) == 0, row, pltpu.roll(tile, 1, 0))

    def from_above(tile, row):
        return jnp.where(row_index(tile.shape[1]) == ROWS - 1, row, pltpu.roll(tile, ROWS - 1, 0))

    first = omega_of(STEPS - 1)

    def keep_faces(kind, value, x, g, cut):
        if g == 0:
            face_y[kind, 0, x : x + 1, cut] = value[:1, :]
        if g == groups - 1:
            face_y[kind, 1, x : x + 1, cut] = value[ROWS - 1 :, :]
        if kind == 0 and x in (0, X - 1):
            if g == 0:
                corner[0 if x == 0 else 1, 0, :, cut] = value[:1, :]
            if g == groups - 1:
                corner[0 if x == 0 else 1, 1, :, cut] = value[ROWS - 1 :, :]

    def prepare(x, g):
        r = slice(g * ROWS, (g + 1) * ROWS)
        up_x, up_y, up_z = beta_ref[0, x, r, :], beta_ref[1, x, r, :], beta_ref[2, x, r, :]
        low_x = rim_x[r, :] if x == 0 else beta_ref[0, x - 1, r, :]
        row = rim_y[x : x + 1, :] if g == 0 else beta_ref[1, x, g * ROWS - 1 : g * ROWS, :]
        low_y = from_below(up_y, row)
        low_z = jnp.where(z_ids == 0, 0.0, pltpu.roll(up_z, 1, 1))
        inv = 1.0 / (up_x + low_x + up_y + low_y + up_z + low_z)
        up_z = jnp.where(z_ids == Z - 1, 0.0, up_z)
        for index, value in enumerate((up_x, low_x, up_y, low_y, up_z, low_z)):
            value = value * inv
            coeff[index, x, r, :] = value
            if index == 3 and g == 0:
                face_coeff[0, x : x + 1, :] = value[:1, :]
                if x in (0, X - 1):
                    near_x[0 if x == 0 else 1, 0] = value[:1, :]
            if index == 2 and g == groups - 1:
                face_coeff[1, x : x + 1, :] = value[ROWS - 1 :, :]
                if x in (0, X - 1):
                    near_x[0 if x == 0 else 1, 1] = value[ROWS - 1 :, :]
            if (index, x) in ((1, 0), (0, X - 1)):
                if g == 0:
                    near_y[0, 1 - index] = value[:1, :]
                if g == groups - 1:
                    near_y[1, 1 - index] = value[ROWS - 1 :, :]
        value = inv * grad_ref[x, r, :]
        target[x, r, :] = value
        value = first * value
        state[0, x, r, :] = value
        keep_faces(0, value, x, g, slice(0, Z))

    def update(kind, omega, x, g, q, par=None):
        source = 1 - kind
        r = slice(g * ROWS, (g + 1) * ROWS)
        cut = slice(q * WIDE, (q + 1) * WIDE)
        start, stop = max(q * WIDE - LANES, 0), min((q + 1) * WIDE + LANES, Z)
        inner = slice(q * WIDE - start, q * WIDE - start + WIDE)
        wide = state[source, x, r, start:stop]
        s = wide[:, inner]
        if g < groups - 1:
            above_row = state[source, x, (g + 1) * ROWS : (g + 1) * ROWS + 1, cut]
        else:
            above_row = 0.0 if par is None else halo_y[par, 1, 1, x : x + 1, cut]
        if g > 0:
            below_row = state[source, x, g * ROWS - 1 : g * ROWS, cut]
        else:
            below_row = 0.0 if par is None else halo_y[par, 1, 0, x : x + 1, cut]
        beside = target[x, r, cut] - s
        beside += coeff[2, x, r, cut] * from_above(s, above_row)
        beside += coeff[3, x, r, cut] * from_below(s, below_row)
        beside += coeff[4, x, r, cut] * pltpu.roll(wide, stop - start - 1, 1)[:, inner]
        beside += coeff[5, x, r, cut] * pltpu.roll(wide, 1, 1)[:, inner]
        if x < X - 1:
            beside += coeff[0, x, r, cut] * state[source, x + 1, r, cut]
        elif par is not None:
            beside += coeff[0, x, r, cut] * halo_x[par, 1, 1, r, cut]
        if x > 0:
            beside += coeff[1, x, r, cut] * state[source, x - 1, r, cut]
        elif par is not None:
            beside += coeff[1, x, r, cut] * halo_x[par, 1, 0, r, cut]
        value = s + omega * beside
        state[kind, x, r, cut] = value
        keep_faces(kind, value, x, g, cut)

    def update_all(kind, omega, q, par=None):
        for x in range(X):
            for g in range(groups):
                update(kind, omega, x, g, q, par)

    def complete_own(par, omega, q):
        cut = slice(q * WIDE, (q + 1) * WIDE)
        for side in sides:
            x = (X - 1) * side
            for g in range(groups):
                r = slice(g * ROWS, (g + 1) * ROWS)
                state[1, x, r, cut] += omega * (coeff[1 - side, x, r, cut] * halo_x[par, 0, side, r, cut])
        for side in sides:
            more = omega * (face_coeff[side, :, cut] * halo_y[par, 0, side, :, cut])
            row = (Y - 1) * side
            for x in range(X):
                state[1, x, row : row + 1, cut] += more[x : x + 1, :]

    def complete_halo(par, omega, q):
        cut = slice(q * WIDE, (q + 1) * WIDE)
        for side in sides:
            x = (X - 1) * side
            for g in range(groups):
                r = slice(g * ROWS, (g + 1) * ROWS)
                halo_x[par, 1, side, r, cut] += omega * (edge_x[side, r, cut] * state[0, x, r, cut])
            for dy in sides:
                row = (Y - 1) * dy
                halo_x[par, 1, side, row : row + 1, cut] += omega * (
                    line_x[side, dy, :, cut] * halo_d[par, side, dy, :, cut])
        for side in sides:
            halo_y[par, 1, side, :, cut] += omega * (edge_y[side, :, cut] * face_y[0, side, :, cut])
            for dx in sides:
                x = (X - 1) * dx
                halo_y[par, 1, side, x : x + 1, cut] += omega * (
                    line_y[side, dx, :, cut] * halo_d[par, dx, side, :, cut])

    loads["grad"].wait()
    for x in range(1, X):
        for g in range(1, groups):
            prepare(x, g)
    (_, rim_x_copy), (_, rim_y_copy) = rim_copies()

    @pl.when(has_x[0])
    def _():
        rim_x_copy.wait_recv()

    for g in range(1, groups):
        prepare(0, g)

    @pl.when(has_y[0])
    def _():
        rim_y_copy.wait_recv()

    for x in range(X):
        prepare(x, 0)

    for q in range(chunks):
        start_sends(0, 0, q)
    for side in sides:
        for has, copy in side_copies(side, 1 - side):
            @pl.when(has)
            def _():
                copy.start()

    for q in range(chunks):
        update_all(1, omega_of(STEPS - 1 - 1 % STEPS), q)
        start_sends(0, 1, q)
        for side in sides:
            @pl.when(has_x[side])
            def _():
                edge_copy(side, q, 1 - side).start()

    for has, copy in rim_copies():
        @pl.when(has[1])
        def _():
            copy.wait_send()

    @pl.loop(1, peers)
    def _(step):
        slot_copy(step).start()

    recv_slots[me] = send_slots[me]

    for side in sides:
        for has, copy in side_copies(side, side):
            @pl.when(has)
            def _():
                copy.wait_recv()

    def round_body(number, carry):
        par = number % 2
        more = number < rounds - 1
        omega = omega_at(2 * number + 1)
        omega_even = omega_at(2 * number + 2)
        omega_odd = omega_at(2 * number + 3)

        def own(q):
            wait_arrivals(par, 0, q)
            wait_sends(1, q)
            complete_own(par, omega, q)

        def odd(q):
            update_all(1, omega_odd, q)
            start_sends(1 - par, 1, q, more)

        own(0)
        for q in range(chunks):
            if q + 1 < chunks:
                own(q + 1)
            wait_arrivals(par, 1, q)
            for side in sides:
                @pl.when(jnp.logical_and(has_x[side], number == 0))
                def _():
                    edge_copy(side, q, side).wait_recv()
            complete_halo(par, omega, q)
            wait_sends(0, q)
            update_all(0, omega_even, q, par)
            start_sends(1 - par, 0, q)
            if q > 0:
                odd(q - 1)
        odd(chunks - 1)
        return carry

    lax.fori_loop(0, rounds, round_body, 0)
    for q in range(chunks):
        wait_arrivals(rounds % 2, 0, q)
        complete_own(rounds % 2, omega_of(STEPS - 1 - (total - 1) % STEPS), q)
    store = pltpu.make_async_copy(state.at[1], out_hbm, load_sem.at[7])
    store.start()
    for q in range(chunks):
        wait_sends(0, q)
    for side in sides:
        for q in range(chunks):
            @pl.when(has_x[side])
            def _():
                edge_copy(side, q, 1 - side).wait_send()
        for has, copy in side_copies(side, 1 - side):
            @pl.when(has)
            def _():
                copy.wait_send()
    for name in ("rows", "mask", "heights"):
        loads[name].wait()

    for x in range(X):
        for b in range(blocks):
            start = (x * blocks + b) * Y
            flat[start : start + Y, :] = state[1, x, :, b * LANES : (b + 1) * LANES]

    unroll = 8

    @pl.loop(0, tiles // unroll)
    def _(chunk):
        for lane in range(unroll):
            t = chunk * unroll + lane
            row = rows_ref[t]
            line = lax.div(row, blocks)
            x = lax.div(line, Y)
            at = (x * blocks + row - line * blocks) * Y + line - x * Y
            picked[pl.ds(t, 1), :] = flat[pl.ds(at, 1), :]

    jumps = picked[...] * mask_ref[...].astype(jnp.float32)
    send_rows[...] = picked_sum(place[...], jumps).reshape(peers, CAP, LANES)

    @pl.loop(1, peers)
    def _(step):
        row_copy(step).start()

    recv_rows[me] = send_rows[me]

    @pl.loop(1, peers)
    def _(step):
        peer, place_of = peer_at(step)
        pltpu.make_async_remote_copy(
            send_slots.at[peer], recv_slots.at[peer], slot_send.at[peer], slot_recv.at[peer],
            device_id=place_of, device_id_type=MESH).wait()

    own = lax.broadcasted_iota(jnp.int32, (peers, CAP, LANES), 1)
    lane_ids = lax.broadcasted_iota(jnp.int32, (peers, CAP, LANES), 2)
    got = jnp.broadcast_to(recv_slots[...], (peers, CAP, LANES))
    slot_of = jnp.sum(jnp.where(own == lane_ids, got, 0.0), axis=2, keepdims=True)
    slot_of = slot_of.reshape(peers * CAP, 1)
    slot_ids = lax.broadcasted_iota(jnp.int32, (peers * CAP, slots), 1).astype(jnp.float32)
    chosen = (slot_of == slot_ids).astype(jnp.float32).T.astype(jnp.bfloat16)

    slope = 0.5 * (heights_ref[2] - heights_ref[0])
    bend = heights_ref[2] - 2.0 * heights_ref[1] + heights_ref[0]
    denom = 1.0 + slope * slope
    factor = 1.0 / (denom * jnp.sqrt(denom))
    skew = -3.0 * slope * bend * factor / denom

    @pl.loop(1, peers)
    def _(step):
        peer, place_of = peer_at(step)
        pltpu.make_async_remote_copy(
            send_rows.at[peer], recv_rows.at[peer], row_send.at[peer], row_recv.at[peer],
            device_id=place_of, device_id_type=MESH).wait()

    table = picked_sum(chosen, recv_rows[...].reshape(peers * CAP, LANES))
    back_ref[0] = table * (factor - 0.5 * skew)
    back_ref[1] = -2.0 * table * factor
    back_ref[2] = table * (factor + 0.5 * skew)
    store.wait()


def shards(grad_pressure, beta, tile_rows, tile_owner, tile_slot, face_mask, heights):
    n_x, n_y = lax.axis_size("gx"), lax.axis_size("gy")
    peers = n_x * n_y
    X, Y, Z = grad_pressure.shape
    chunks = Z // WIDE
    tiles = tile_rows.shape[0]
    f32 = jnp.float32
    vmem = pl.BlockSpec(memory_space=pltpu.VMEM)
    hbm = pl.BlockSpec(memory_space=pltpu.HBM)
    dma = pltpu.SemaphoreType.DMA
    return pl.pallas_call(
        functools.partial(kernel, n_x, n_y),
        out_shape=(
            jax.ShapeDtypeStruct((X, Y, Z), f32),
            jax.ShapeDtypeStruct(heights.shape, f32),
        ),
        in_specs=[hbm] * 7,
        out_specs=(hbm, vmem),
        scratch_shapes=[
            pltpu.VMEM((X, Y, Z), f32),
            pltpu.VMEM(beta.shape, f32),
            pltpu.SMEM((tiles,), jnp.int32),
            pltpu.VMEM((1, tiles), jnp.int32),
            pltpu.VMEM((1, tiles), jnp.int32),
            pltpu.VMEM(face_mask.shape, jnp.int32),
            pltpu.VMEM(heights.shape, f32),
            dma((8,)),
            pltpu.VMEM((6, X, Y, Z), f32),
            pltpu.VMEM((X, Y, Z), f32),
            pltpu.VMEM((2, X, Y, Z), f32),
            pltpu.VMEM((2, 2, X, Z), f32),
            pltpu.VMEM((2, 2, 1, Z), f32),
            pltpu.VMEM((2, 2, 2, Y, Z), f32),
            pltpu.VMEM((2, 2, 2, X, Z), f32),
            pltpu.VMEM((2, 2, 2, 1, Z), f32),
            pltpu.VMEM((Y, Z), f32),
            pltpu.VMEM((X, Z), f32),
            pltpu.VMEM((X, Z), f32),
            pltpu.VMEM((2, X, Z), f32),
            pltpu.VMEM((2, Y, Z), f32),
            pltpu.VMEM((2, X, Z), f32),
            pltpu.VMEM((2, 2, 1, Z), f32),
            pltpu.VMEM((2, 2, 1, Z), f32),
            pltpu.VMEM((2, 2, 1, Z), f32),
            pltpu.VMEM((2, 2, 1, Z), f32),
            pltpu.VMEM((X * Y * Z // LANES, LANES), f32),
            pltpu.VMEM((tiles, LANES), f32),
            pltpu.VMEM((peers * CAP, tiles), jnp.bfloat16),
            pltpu.VMEM((peers, CAP, LANES), f32),
            pltpu.VMEM((peers, CAP, LANES), f32),
            pltpu.VMEM((peers, 1, LANES), f32),
            pltpu.VMEM((peers, 1, LANES), f32),
            dma((2,)),
            dma((2,)),
            dma((2, 2, chunks)),
            dma((2, 2, 2, chunks)),
            dma((2, 2, chunks)),
            dma((2, 2, 2, chunks)),
            dma((2, 2, chunks)),
            dma((2, 2, 2, chunks)),
            dma((2, chunks)),
            dma((2, chunks)),
            dma((3, 2)),
            dma((3, 2)),
            dma((peers,)),
            dma((peers,)),
            dma((peers,)),
            dma((peers,)),
        ],
        compiler_params=pltpu.CompilerParams(
            collective_id=0, has_side_effects=True, vmem_limit_bytes=56 * 1024 * 1024
        ),
    )(grad_pressure, beta, tile_rows, tile_owner.reshape(1, -1), tile_slot.reshape(1, -1), face_mask, heights)


def solution(mesh):
    in_specs = (
        P("gx", "gy", None),
        P(None, "gx", "gy", None),
        P(("gx", "gy")),
        P(("gx", "gy"), None),
        P(("gx", "gy")),
        P(("gx", "gy"), None),
        P(None, ("gx", "gy"), None),
    )
    out_specs = (P("gx", "gy", None), P(None, ("gx", "gy"), None))
    return jax.shard_map(shards, mesh=mesh, in_specs=in_specs, out_specs=out_specs, check_vma=False)
```

time: 62.3 us -> 56.5 us (0.907)
  Pallas kernels: 57.4 us -> 51.6 us
    pallas_call x1, Pallas kernels: 57.4 us -> 51.6 us  [shards(): pl.pallas_call(functools.partial(kernel, n_x, n_y), out_shape=(jax.ShapeD...]
where the time goes in v1:
time: 56.5 us; the launch traced here: 56.3 us
  Pallas kernels  51.6 us (91%)
  local copies, waits for them, and re-layouts  4.07 us (7%)
  between operations  0.64 us (1%)
    pallas_call x1, Pallas kernels, shards(): pl.pallas_call(functools.partial(kernel, n_x, n_y), out_shape=(jax.ShapeD...  51.6 us
    unnamed x2, local copies, waits for them, and re-layouts  4.07 us

profile of v1, /device:TPU:0, one launch (start us, length us, event | category | flops | bytes accessed | tf_op | source)
XLA Modules:
  0.0 56.3 jit_solution(10694522393841608068)
XLA Ops:
  0.6 51.6 %shard_map.86 = (f32[8,32,1024]{2,1,0:T(8,128)}, f32[3,256,128]{2,1,0:T(8,128)}) custom-call(f32[8,32,1024]{2,1,0:T(8,128)} %grad_in.1, f32[3,8,32,1024]{3,2,1,0:T(8,128)} %beta_in.1, s32[256]{0:T(256)} %rows_in.1, s32[1,256]{1,0:T(1,128)} %bitcast.2, s32[1,256]{1,0:T(1,128)} %bitcast.3, s32[256,128]{1,0:T(8,128)} %mask_in.1, f32[3,256,128]{2,1,0:T(8,128)} %heights_in.1), custom_call_target="tpu_custom_call" | custom-call | tf_op jit(solution)/shard_map/pallas_call | solution.py:521
  52.3 2.3 %copy.11 = f32[8,32,1024]{2,1,0:T(8,128)} copy(f32[8,32,1024]{2,1,0:T(8,128)} %get-tuple-element.4) | data formatting | bytes 2097152
  54.6 1.8 %copy.12 = f32[3,256,128]{2,1,0:T(8,128)} copy(f32[3,256,128]{2,1,0:T(8,128)} %get-tuple-element.5) | data formatting | bytes 786432

commit v2 on v1

--- a/solution.py
+++ b/solution.py
@@ -13,6 +13,7 @@
 CAP = 8
 LANES = 128
 ROWS = 8
+UNROLL = 16
 WIDE = 256
 
 LOW_BOUND = 0.1
@@ -49,11 +50,11 @@
 def kernel(
     n_x, n_y,
     grad_in, beta_in, rows_in, owner_in, slot_in, mask_in, heights_in,
-    out_hbm, back_ref,
+    out_ref, back_ref,
     grad_ref, beta_ref, rows_ref, owner_ref, slot_ref, mask_ref, heights_ref, load_sem,
     coeff, target, state, face_y, corner, halo_x, halo_y, halo_d,
     rim_x, rim_y, rim_face, face_coeff, edge_x, edge_y, near_x, near_y, line_x, line_y,
-    flat, picked, place, send_rows, recv_rows, send_slots, recv_slots,
+    flat, picked, spots_ref, chosen, scales, place, send_rows, recv_rows, send_slots, recv_slots,
     rim_send, rim_recv, x_send, x_recv, y_send, y_recv, d_send, d_recv,
     edge_send, edge_recv, side_send, side_recv, row_send, row_recv, slot_send, slot_recv,
 ):
@@ -428,50 +429,17 @@
         return carry
 
     lax.fori_loop(0, rounds, round_body, 0)
-    for q in range(chunks):
-        wait_arrivals(rounds % 2, 0, q)
-        complete_own(rounds % 2, omega_of(STEPS - 1 - (total - 1) % STEPS), q)
-    store = pltpu.make_async_copy(state.at[1], out_hbm, load_sem.at[7])
-    store.start()
-    for q in range(chunks):
-        wait_sends(0, q)
-    for side in sides:
-        for q in range(chunks):
-            @pl.when(has_x[side])
-            def _():
-                edge_copy(side, q, 1 - side).wait_send()
-        for has, copy in side_copies(side, 1 - side):
-            @pl.when(has)
-            def _():
-                copy.wait_send()
     for name in ("rows", "mask", "heights"):
         loads[name].wait()
 
-    for x in range(X):
-        for b in range(blocks):
-            start = (x * blocks + b) * Y
-            flat[start : start + Y, :] = state[1, x, :, b * LANES : (b + 1) * LANES]
-
-    unroll = 8
-
-    @pl.loop(0, tiles // unroll)
-    def _(chunk):
-        for lane in range(unroll):
-            t = chunk * unroll + lane
+    @pl.loop(0, tiles // UNROLL)
+    def _(part):
+        for lane in range(UNROLL):
+            t = part * UNROLL + lane
             row = rows_ref[t]
             line = lax.div(row, blocks)
             x = lax.div(line, Y)
-            at = (x * blocks + row - line * blocks) * Y + line - x * Y
-            picked[pl.ds(t, 1), :] = flat[pl.ds(at, 1), :]
-
-    jumps = picked[...] * mask_ref[...].astype(jnp.float32)
-    send_rows[...] = picked_sum(place[...], jumps).reshape(peers, CAP, LANES)
-
-    @pl.loop(1, peers)
-    def _(step):
-        row_copy(step).start()
-
-    recv_rows[me] = send_rows[me]
+            spots_ref[t] = (x * blocks + row - line * blocks) * Y + line - x * Y
 
     @pl.loop(1, peers)
     def _(step):
@@ -486,13 +454,52 @@
     slot_of = jnp.sum(jnp.where(own == lane_ids, got, 0.0), axis=2, keepdims=True)
     slot_of = slot_of.reshape(peers * CAP, 1)
     slot_ids = lax.broadcasted_iota(jnp.int32, (peers * CAP, slots), 1).astype(jnp.float32)
-    chosen = (slot_of == slot_ids).astype(jnp.float32).T.astype(jnp.bfloat16)
+    chosen[...] = (slot_of == slot_ids).astype(jnp.float32).T.astype(jnp.bfloat16)
 
     slope = 0.5 * (heights_ref[2] - heights_ref[0])
     bend = heights_ref[2] - 2.0 * heights_ref[1] + heights_ref[0]
     denom = 1.0 + slope * slope
     factor = 1.0 / (denom * jnp.sqrt(denom))
     skew = -3.0 * slope * bend * factor / denom
+    scales[0] = factor - 0.5 * skew
+    scales[1] = -2.0 * factor
+    scales[2] = factor + 0.5 * skew
+
+    for q in range(chunks):
+        wait_arrivals(rounds % 2, 0, q)
+        complete_own(rounds % 2, omega_of(STEPS - 1 - (total - 1) % STEPS), q)
+    for q in range(chunks):
+        wait_sends(0, q)
+    for side in sides:
+        for q in range(chunks):
+            @pl.when(has_x[side])
+            def _():
+                edge_copy(side, q, 1 - side).wait_send()
+        for has, copy in side_copies(side, 1 - side):
+            @pl.when(has)
+            def _():
+                copy.wait_send()
+    for x in range(X):
+        for b in range(blocks):
+            start = (x * blocks + b) * Y
+            value = state[1, x, :, b * LANES : (b + 1) * LANES]
+            flat[start : start + Y, :] = value
+            out_ref[x, :, b * LANES : (b + 1) * LANES] = value
+
+    @pl.loop(0, tiles // UNROLL)
+    def _(part):
+        for lane in range(UNROLL):
+            t = part * UNROLL + lane
+            picked[pl.ds(t, 1), :] = flat[pl.ds(spots_ref[t], 1), :]
+
+    jumps = picked[...] * mask_ref[...].astype(jnp.float32)
+    send_rows[...] = picked_sum(place[...], jumps).reshape(peers, CAP, LANES)
+
+    @pl.loop(1, peers)
+    def _(step):
+        row_copy(step).start()
+
+    recv_rows[me] = send_rows[me]
 
     @pl.loop(1, peers)
     def _(step):
@@ -501,11 +508,20 @@
             send_rows.at[peer], recv_rows.at[peer], row_send.at[peer], row_recv.at[peer],
             device_id=place_of, device_id_type=MESH).wait()
 
-    table = picked_sum(chosen, recv_rows[...].reshape(peers * CAP, LANES))
-    back_ref[0] = table * (factor - 0.5 * skew)
-    back_ref[1] = -2.0 * table * factor
-    back_ref[2] = table * (factor + 0.5 * skew)
-    store.wait()
+    table = picked_sum(chosen[...], recv_rows[...].reshape(peers * CAP, LANES))
+    for index in range(3):
+        back_ref[index] = table * scales[index]
+
+
+def hand_over(first_held, second_held, first_out, second_out, sem):
+    stores = []
+    for held, landing in ((first_held, first_out), (second_held, second_out)):
+        for index in range(held.shape[0]):
+            stores.append(pltpu.make_async_copy(held.at[index], landing.at[index], sem.at[len(stores)]))
+    for store in stores:
+        store.start()
+    for store in stores:
+        store.wait()
 
 
 def shards(grad_pressure, beta, tile_rows, tile_owner, tile_slot, face_mask, heights):
@@ -518,14 +534,11 @@
     vmem = pl.BlockSpec(memory_space=pltpu.VMEM)
     hbm = pl.BlockSpec(memory_space=pltpu.HBM)
     dma = pltpu.SemaphoreType.DMA
-    return pl.pallas_call(
+    results = pl.pallas_call(
         functools.partial(kernel, n_x, n_y),
-        out_shape=(
-            jax.ShapeDtypeStruct((X, Y, Z), f32),
-            jax.ShapeDtypeStruct(heights.shape, f32),
-        ),
+        out_shape=(pltpu.VMEM((X, Y, Z), f32), pltpu.VMEM(heights.shape, f32)),
         in_specs=[hbm] * 7,
-        out_specs=(hbm, vmem),
+        out_specs=(vmem, vmem),
         scratch_shapes=[
             pltpu.VMEM((X, Y, Z), f32),
             pltpu.VMEM(beta.shape, f32),
@@ -555,6 +568,9 @@
             pltpu.VMEM((2, 2, 1, Z), f32),
             pltpu.VMEM((X * Y * Z // LANES, LANES), f32),
             pltpu.VMEM((tiles, LANES), f32),
+            pltpu.SMEM((tiles,), jnp.int32),
+            pltpu.VMEM((heights.shape[1], peers * CAP), jnp.bfloat16),
+            pltpu.VMEM(heights.shape, f32),
             pltpu.VMEM((peers * CAP, tiles), jnp.bfloat16),
             pltpu.VMEM((peers, CAP, LANES), f32),
             pltpu.VMEM((peers, CAP, LANES), f32),
@@ -578,9 +594,17 @@
             dma((peers,)),
         ],
         compiler_params=pltpu.CompilerParams(
-            collective_id=0, has_side_effects=True, vmem_limit_bytes=56 * 1024 * 1024
+            collective_id=0, has_side_effects=True, vmem_limit_bytes=60 * 1024 * 1024
         ),
     )(grad_pressure, beta, tile_rows, tile_owner.reshape(1, -1), tile_slot.reshape(1, -1), face_mask, heights)
+    parts = sum(result.shape[0] for result in results)
+    return pl.pallas_call(
+        hand_over,
+        out_shape=tuple(jax.ShapeDtypeStruct(result.shape, f32) for result in results),
+        in_specs=[vmem] * 2,
+        out_specs=(hbm, hbm),
+        scratch_shapes=[dma((parts,))],
+    )(*[pltpu.with_memory_space_constraint(result, pltpu.VMEM) for result in results])
 
 
 def solution(mesh):

time: 56.5 us -> 51.5 us (0.912)
  local copies, waits for them, and re-layouts: 4.07 us -> 0 us
  Pallas kernels: 51.6 us -> 50.7 us
    unnamed x2 -> x0, local copies, waits for them, and re-layouts: 4.07 us -> none
    pallas_call x1 -> x2, Pallas kernels: 51.6 us -> 50.7 us  [the longest x1 49.5 us: shards(): pl.pallas_call(functools.partial(kernel, n_x, n_y), out_shape=(pltpu.VMEM...]
where the time goes in v2:
time: 51.5 us; the launch traced here: 51.3 us
  Pallas kernels  50.7 us (98%)
  between operations  0.64 us (1%)
    pallas_call x1, Pallas kernels, shards(): pl.pallas_call(functools.partial(kernel, n_x, n_y), out_shape=(pltpu.VMEM...  49.5 us
    pallas_call x1, Pallas kernels, shards(): pl.pallas_call(hand_over, out_shape=tuple((jax.ShapeDtypeStruct(result.sh...  1.18 us

profile of v2, /device:TPU:0, one launch (start us, length us, event | category | flops | bytes accessed | tf_op | source)
XLA Modules:
  0.0 51.3 jit_solution(7333856905069005003)
XLA Ops:
  0.6 49.5 %shard_map.86 = (f32[8,32,1024]{2,1,0:T(8,128)S(1)}, f32[3,256,128]{2,1,0:T(8,128)S(1)}) custom-call(f32[8,32,1024]{2,1,0:T(8,128)} %grad_in.1, f32[3,8,32,1024]{3,2,1,0:T(8,128)} %beta_in.1, s32[256]{0:T(256)} %rows_in.1, s32[1,256]{1,0:T(1,128)} %bitcast.2, s32[1,256]{1,0:T(1,128)} %bitcast.3, s32[256,128]{1,0:T(8,128)} %mask_in.1, f32[3,256,128]{2,1,0:T(8,128)} %heights_in.1), custom_call_target="tpu_custom_call" | custom-call | tf_op jit(solution)/shard_map/pallas_call | solution.py:537
  50.1 1.2 %shard_map.87 = (f32[8,32,1024]{2,1,0:T(8,128)}, f32[3,256,128]{2,1,0:T(8,128)}) custom-call(f32[8,32,1024]{2,1,0:T(8,128)S(1)} %get-tuple-element.4.first_held, f32[3,256,128]{2,1,0:T(8,128)S(1)} %get-tuple-element.5.second_held), custom_call_target="tpu_custom_call" | custom-call | tf_op jit(solution)/shard_map/pallas_call | solution.py:601

commit v3 on v2

--- a/solution.py
+++ b/solution.py
@@ -53,10 +53,11 @@
     out_ref, back_ref,
     grad_ref, beta_ref, rows_ref, owner_ref, slot_ref, mask_ref, heights_ref, load_sem,
     coeff, target, state, face_y, corner, halo_x, halo_y, halo_d,
-    rim_x, rim_y, rim_face, face_coeff, edge_x, edge_y, near_x, near_y, line_x, line_y,
+    rim_x, rim_y, rim_face, face_coeff, edge_x, edge_y, line_x, line_y,
+    part_x, part_y, grad_y, near_x, near_y, near_d, raw_x, raw_y, raw_by, raw_bx, raw_d,
     flat, picked, spots_ref, chosen, scales, place, send_rows, recv_rows, send_slots, recv_slots,
-    rim_send, rim_recv, x_send, x_recv, y_send, y_recv, d_send, d_recv,
-    edge_send, edge_recv, side_send, side_recv, row_send, row_recv, slot_send, slot_recv,
+    x_send, x_recv, y_send, y_recv, d_send, d_recv,
+    raw_send, raw_recv, lone_send, lone_recv, row_send, row_recv, slot_send, slot_recv,
 ):
     X, Y, Z = grad_ref.shape
     groups = Y // ROWS
@@ -76,7 +77,7 @@
     total = ITERS * STEPS
     rounds = (total - 2) // 2
 
-    for ref in (rim_x, rim_y, halo_x, halo_y, halo_d, edge_x, edge_y, line_x, line_y):
+    for ref in (rim_x, rim_y, halo_x, halo_y, halo_d, edge_x, edge_y, line_x, line_y, raw_d):
         ref[...] = jnp.zeros_like(ref)
 
     def peer_at(step):
@@ -122,25 +123,51 @@
     )
     send_slots[...] = slot_rows.reshape(peers, 1, LANES)
 
+    z_ids = lax.broadcasted_iota(jnp.int32, (ROWS, Z), 1)
+
+    def row_index(width):
+        return lax.broadcasted_iota(jnp.int32, (ROWS, width), 0)
+
+    def from_below(tile, row):
+        return jnp.where(row_index(tile.shape[1]) == 0, row, pltpu.roll(tile, 1, 0))
+
+    def from_above(tile, row):
+        return jnp.where(row_index(tile.shape[1]) == ROWS - 1, row, pltpu.roll(tile, ROWS - 1, 0))
+
+    def part_of_diagonal(x, g):
+        r = slice(g * ROWS, (g + 1) * ROWS)
+        up_y, up_z = beta_ref[1, x, r, :], beta_ref[2, x, r, :]
+        low_y = from_below(up_y, 0.0 if g == 0 else beta_ref[1, x, g * ROWS - 1 : g * ROWS, :])
+        value = beta_ref[0, x, r, :] + up_y + low_y + up_z + jnp.where(z_ids == 0, 0.0, pltpu.roll(up_z, 1, 1))
+        return value if x == 0 else value + beta_ref[0, x - 1, r, :]
+
     loads["beta"].wait()
     for x in range(X):
         rim_face[x : x + 1, :] = beta_ref[1, x, Y - 1 : Y, :]
+        for g in range(groups):
+            if x in (0, X - 1) or g in (0, groups - 1):
+                value = part_of_diagonal(x, g)
+                if x in (0, X - 1):
+                    part_x[0 if x == 0 else 1, g * ROWS : (g + 1) * ROWS, :] = value
+                if g == 0:
+                    part_y[0, x : x + 1, :] = value[:1, :]
+                if g == groups - 1:
+                    part_y[1, x : x + 1, :] = value[ROWS - 1 :, :]
+    for side in sides:
+        near_x[side] = beta_ref[1, (X - 1) * side, Y - 1 : Y, :]
+        near_y[side] = beta_ref[0, X - 1, (Y - 1) * side : (Y - 1) * side + 1, :]
+        for dy in sides:
+            near_d[side, dy, 0] = beta_ref[0, X - 1, (Y - 1) * dy : (Y - 1) * dy + 1, :]
+            near_d[side, dy, 1] = beta_ref[1, (X - 1) * side, Y - 1 : Y, :]
+    loads["grad"].wait()
+    for x in range(X):
+        for side in sides:
+            grad_y[side, x : x + 1, :] = grad_ref[x, (Y - 1) * side : (Y - 1) * side + 1, :]
 
     pl.semaphore_wait(barrier, peers - 1)
 
     def remote(source, landing, send, recv, place_of):
         return pltpu.make_async_remote_copy(source, landing, send, recv, device_id=place_of, device_id_type=MESH)
-
-    def rim_copies():
-        return (
-            (has_x, remote(beta_ref.at[0, X - 1], rim_x, rim_send.at[0], rim_recv.at[0], at_x[1])),
-            (has_y, remote(rim_face, rim_y, rim_send.at[1], rim_recv.at[1], at_y[1])),
-        )
-
-    for has, copy in rim_copies():
-        @pl.when(has[1])
-        def _():
-            copy.start()
 
     def slot_copy(step):
         peer, place_of = peer_at(step)
@@ -205,28 +232,37 @@
             def _():
                 copy.wait_recv()
 
-    def edge_copy(side, q, land):
-        return remote(
-            coeff.at[1 - side, (X - 1) * side, :, lanes(q)], edge_x.at[land, :, lanes(q)],
-            edge_send.at[side, q], edge_recv.at[land, q], at_x[side])
-
-    def side_copies(side, land):
-        return (
-            (has_y[side], remote(face_coeff.at[side], edge_y.at[land], side_send.at[0, side], side_recv.at[0, land], at_y[side])),
-            (has_x[side], remote(near_x.at[side], line_x.at[land], side_send.at[1, side], side_recv.at[1, land], at_x[side])),
-            (has_y[side], remote(near_y.at[side], line_y.at[land], side_send.at[2, side], side_recv.at[2, land], at_y[side])),
-        )
-
-    def row_index(width):
-        return lax.broadcasted_iota(jnp.int32, (ROWS, width), 0)
-
-    z_ids = lax.broadcasted_iota(jnp.int32, (ROWS, Z), 1)
-
-    def from_below(tile, row):
-        return jnp.where(row_index(tile.shape[1]) == 0, row, pltpu.roll(tile, 1, 0))
-
-    def from_above(tile, row):
-        return jnp.where(row_index(tile.shape[1]) == ROWS - 1, row, pltpu.roll(tile, ROWS - 1, 0))
+    def lone_copies(side, arriving):
+        land = side if arriving else 1 - side
+        found = [
+            (has_x[side], remote(near_x.at[side], raw_by.at[land], lone_send.at[0, side], lone_recv.at[0, land], at_x[side])),
+            (has_y[side], remote(near_y.at[side], raw_bx.at[land], lone_send.at[1, side], lone_recv.at[1, land], at_y[side])),
+        ]
+        for dy in sides:
+            other = dy if arriving else 1 - dy
+            found.append((jnp.logical_and(has_x[side], has_y[dy]), remote(
+                near_d.at[side, dy], raw_d.at[land, other], lone_send.at[2 + dy, side], lone_recv.at[2 + other, land],
+                (at_x[side][0], at_y[dy][1]))))
+        return found
+
+    def raw_copies(q, arriving):
+        cut = lanes(q)
+        found = []
+        for side in sides:
+            land = side if arriving else 1 - side
+            sources = (
+                (has_x, at_x, 0, beta_ref.at[0, X - 1, :, cut], rim_x.at[:, cut]),
+                (has_y, at_y, 1, rim_face.at[:, cut], rim_y.at[:, cut]),
+                (has_x, at_x, 2, grad_ref.at[(X - 1) * side, :, cut], raw_x.at[0, land, :, cut]),
+                (has_y, at_y, 3, grad_y.at[side, :, cut], raw_y.at[0, land, :, cut]),
+                (has_x, at_x, 4, part_x.at[side, :, cut], raw_x.at[1, land, :, cut]),
+                (has_y, at_y, 5, part_y.at[side, :, cut], raw_y.at[1, land, :, cut]),
+            )
+            for has, at, kind, source, landing in sources:
+                if kind > 1 or side == (0 if arriving else 1):
+                    found.append((has[side], remote(
+                        source, landing, raw_send.at[kind, side, q], raw_recv.at[kind, land, q], at[side])))
+        return found
 
     first = omega_of(STEPS - 1)
 
@@ -241,36 +277,63 @@
             if g == groups - 1:
                 corner[0 if x == 0 else 1, 1, :, cut] = value[ROWS - 1 :, :]
 
-    def prepare(x, g):
+    def prepare(x, g, q=None):
         r = slice(g * ROWS, (g + 1) * ROWS)
-        up_x, up_y, up_z = beta_ref[0, x, r, :], beta_ref[1, x, r, :], beta_ref[2, x, r, :]
-        low_x = rim_x[r, :] if x == 0 else beta_ref[0, x - 1, r, :]
-        row = rim_y[x : x + 1, :] if g == 0 else beta_ref[1, x, g * ROWS - 1 : g * ROWS, :]
+        start, stop = (0, Z) if q is None else (q * WIDE, (q + 1) * WIDE)
+        cut = slice(start, stop)
+        wide = slice(max(start - LANES, 0), stop)
+        inner = slice(start - wide.start, stop - wide.start)
+        z_at = z_ids[:, cut]
+        up_x, up_y, up_z = beta_ref[0, x, r, cut], beta_ref[1, x, r, cut], beta_ref[2, x, r, wide]
+        low_x = rim_x[r, cut] if x == 0 else beta_ref[0, x - 1, r, cut]
+        row = rim_y[x : x + 1, cut] if g == 0 else beta_ref[1, x, g * ROWS - 1 : g * ROWS, cut]
         low_y = from_below(up_y, row)
-        low_z = jnp.where(z_ids == 0, 0.0, pltpu.roll(up_z, 1, 1))
+        low_z = jnp.where(z_at == 0, 0.0, pltpu.roll(up_z, 1, 1)[:, inner])
+        up_z = up_z[:, inner]
         inv = 1.0 / (up_x + low_x + up_y + low_y + up_z + low_z)
-        up_z = jnp.where(z_ids == Z - 1, 0.0, up_z)
+        up_z = jnp.where(z_at == Z - 1, 0.0, up_z)
         for index, value in enumerate((up_x, low_x, up_y, low_y, up_z, low_z)):
             value = value * inv
-            coeff[index, x, r, :] = value
+            coeff[index, x, r, cut] = value
             if index == 3 and g == 0:
-                face_coeff[0, x : x + 1, :] = value[:1, :]
-                if x in (0, X - 1):
-                    near_x[0 if x == 0 else 1, 0] = value[:1, :]
+                face_coeff[0, x : x + 1, cut] = value[:1, :]
             if index == 2 and g == groups - 1:
-                face_coeff[1, x : x + 1, :] = value[ROWS - 1 :, :]
-                if x in (0, X - 1):
-                    near_x[0 if x == 0 else 1, 1] = value[ROWS - 1 :, :]
-            if (index, x) in ((1, 0), (0, X - 1)):
-                if g == 0:
-                    near_y[0, 1 - index] = value[:1, :]
-                if g == groups - 1:
-                    near_y[1, 1 - index] = value[ROWS - 1 :, :]
-        value = inv * grad_ref[x, r, :]
-        target[x, r, :] = value
-        value = first * value
-        state[0, x, r, :] = value
-        keep_faces(0, value, x, g, slice(0, Z))
+                face_coeff[1, x : x + 1, cut] = value[ROWS - 1 :, :]
+        value = inv * grad_ref[x, r, cut]
+        target[x, r, cut] = value
+        state[1, x, r, cut] = first * value
+
+    def prepare_halo_x(side, q):
+        cut = slice(q * WIDE, (q + 1) * WIDE)
+        for g in range(groups):
+            r = slice(g * ROWS, (g + 1) * ROWS)
+            shared = beta_ref[0, X - 1, r, cut] if side else rim_x[r, cut]
+            total_of = raw_x[1, side, r, cut]
+            if side:
+                total_of += shared
+            if g == 0:
+                total_of += jnp.where(row_index(WIDE) == 0, raw_d[side, 0, 1, :, cut], 0.0)
+            inv = 1.0 / total_of
+            halo_x[1, 1, side, r, cut] = first * (inv * raw_x[0, side, r, cut])
+            edge_x[side, r, cut] = shared * inv
+            if g == 0:
+                line_x[side, 0, :, cut] = raw_d[side, 0, 1, :, cut] * inv[:1, :]
+            if g == groups - 1:
+                line_x[side, 1, :, cut] = raw_by[side, :, cut] * inv[ROWS - 1 :, :]
+
+    def prepare_halo_y(side, q):
+        cut = slice(q * WIDE, (q + 1) * WIDE)
+        shared = rim_face[:, cut] if side else rim_y[:, cut]
+        total_of = raw_y[1, side, :, cut]
+        if side:
+            total_of += shared
+        planes = lax.broadcasted_iota(jnp.int32, (X, WIDE), 0)
+        total_of += jnp.where(planes == 0, raw_d[0, side, 0, :, cut], 0.0)
+        inv = 1.0 / total_of
+        halo_y[1, 1, side, :, cut] = first * (inv * raw_y[0, side, :, cut])
+        edge_y[side, :, cut] = shared * inv
+        line_y[side, 0, :, cut] = raw_d[0, side, 0, :, cut] * inv[:1, :]
+        line_y[side, 1, :, cut] = raw_bx[side, :, cut] * inv[X - 1 :, :]
 
     def update(kind, omega, x, g, q, par=None):
         source = 1 - kind
@@ -341,94 +404,26 @@
                 halo_y[par, 1, side, x : x + 1, cut] += omega * (
                     line_y[side, dx, :, cut] * halo_d[par, dx, side, :, cut])
 
-    loads["grad"].wait()
+    for side in sides:
+        for has, copy in lone_copies(side, False):
+            @pl.when(has)
+            def _():
+                copy.start()
+    for q in range(chunks):
+        for has, copy in raw_copies(q, False):
+            @pl.when(has)
+            def _():
+                copy.start()
+
+    @pl.loop(1, peers)
+    def _(step):
+        slot_copy(step).start()
+
+    recv_slots[me] = send_slots[me]
     for x in range(1, X):
         for g in range(1, groups):
             prepare(x, g)
-    (_, rim_x_copy), (_, rim_y_copy) = rim_copies()
-
-    @pl.when(has_x[0])
-    def _():
-        rim_x_copy.wait_recv()
-
-    for g in range(1, groups):
-        prepare(0, g)
-
-    @pl.when(has_y[0])
-    def _():
-        rim_y_copy.wait_recv()
-
-    for x in range(X):
-        prepare(x, 0)
-
-    for q in range(chunks):
-        start_sends(0, 0, q)
-    for side in sides:
-        for has, copy in side_copies(side, 1 - side):
-            @pl.when(has)
-            def _():
-                copy.start()
-
-    for q in range(chunks):
-        update_all(1, omega_of(STEPS - 1 - 1 % STEPS), q)
-        start_sends(0, 1, q)
-        for side in sides:
-            @pl.when(has_x[side])
-            def _():
-                edge_copy(side, q, 1 - side).start()
-
-    for has, copy in rim_copies():
-        @pl.when(has[1])
-        def _():
-            copy.wait_send()
-
-    @pl.loop(1, peers)
-    def _(step):
-        slot_copy(step).start()
-
-    recv_slots[me] = send_slots[me]
-
-    for side in sides:
-        for has, copy in side_copies(side, side):
-            @pl.when(has)
-            def _():
-                copy.wait_recv()
-
-    def round_body(number, carry):
-        par = number % 2
-        more = number < rounds - 1
-        omega = omega_at(2 * number + 1)
-        omega_even = omega_at(2 * number + 2)
-        omega_odd = omega_at(2 * number + 3)
-
-        def own(q):
-            wait_arrivals(par, 0, q)
-            wait_sends(1, q)
-            complete_own(par, omega, q)
-
-        def odd(q):
-            update_all(1, omega_odd, q)
-            start_sends(1 - par, 1, q, more)
-
-        own(0)
-        for q in range(chunks):
-            if q + 1 < chunks:
-                own(q + 1)
-            wait_arrivals(par, 1, q)
-            for side in sides:
-                @pl.when(jnp.logical_and(has_x[side], number == 0))
-                def _():
-                    edge_copy(side, q, side).wait_recv()
-            complete_halo(par, omega, q)
-            wait_sends(0, q)
-            update_all(0, omega_even, q, par)
-            start_sends(1 - par, 0, q)
-            if q > 0:
-                odd(q - 1)
-        odd(chunks - 1)
-        return carry
-
-    lax.fori_loop(0, rounds, round_body, 0)
+
     for name in ("rows", "mask", "heights"):
         loads[name].wait()
 
@@ -441,21 +436,6 @@
             x = lax.div(line, Y)
             spots_ref[t] = (x * blocks + row - line * blocks) * Y + line - x * Y
 
-    @pl.loop(1, peers)
-    def _(step):
-        peer, place_of = peer_at(step)
-        pltpu.make_async_remote_copy(
-            send_slots.at[peer], recv_slots.at[peer], slot_send.at[peer], slot_recv.at[peer],
-            device_id=place_of, device_id_type=MESH).wait()
-
-    own = lax.broadcasted_iota(jnp.int32, (peers, CAP, LANES), 1)
-    lane_ids = lax.broadcasted_iota(jnp.int32, (peers, CAP, LANES), 2)
-    got = jnp.broadcast_to(recv_slots[...], (peers, CAP, LANES))
-    slot_of = jnp.sum(jnp.where(own == lane_ids, got, 0.0), axis=2, keepdims=True)
-    slot_of = slot_of.reshape(peers * CAP, 1)
-    slot_ids = lax.broadcasted_iota(jnp.int32, (peers * CAP, slots), 1).astype(jnp.float32)
-    chosen[...] = (slot_of == slot_ids).astype(jnp.float32).T.astype(jnp.bfloat16)
-
     slope = 0.5 * (heights_ref[2] - heights_ref[0])
     bend = heights_ref[2] - 2.0 * heights_ref[1] + heights_ref[0]
     denom = 1.0 + slope * slope
@@ -465,24 +445,93 @@
     scales[1] = -2.0 * factor
     scales[2] = factor + 0.5 * skew
 
+    for side in sides:
+        for has, copy in lone_copies(side, True):
+            @pl.when(has)
+            def _():
+                copy.wait_recv()
+
+    def begin(q):
+        for has, copy in raw_copies(q, True):
+            @pl.when(has)
+            def _():
+                copy.wait_recv()
+        for g in range(1, groups):
+            prepare(0, g, q)
+        for x in range(X):
+            prepare(x, 0, q)
+        for side in sides:
+            @pl.when(has_x[side])
+            def _():
+                prepare_halo_x(side, q)
+
+            @pl.when(has_y[side])
+            def _():
+                prepare_halo_y(side, q)
+
+    def second(q):
+        update_all(1, omega_of(STEPS - 1 - 2 % STEPS), q)
+        start_sends(0, 1, q)
+
+    begin(0)
     for q in range(chunks):
-        wait_arrivals(rounds % 2, 0, q)
-        complete_own(rounds % 2, omega_of(STEPS - 1 - (total - 1) % STEPS), q)
+        if q + 1 < chunks:
+            begin(q + 1)
+        update_all(0, omega_of(STEPS - 1 - 1 % STEPS), q, 1)
+        start_sends(0, 0, q)
+        if q > 0:
+            second(q - 1)
+    second(chunks - 1)
+
+    def round_body(number, carry):
+        par = number % 2
+        more = number < rounds - 1
+        omega = omega_at(2 * number + 2)
+        omega_even = omega_at(2 * number + 3)
+        omega_odd = omega_at(2 * number + 4)
+
+        def own(q):
+            wait_arrivals(par, 0, q)
+            wait_sends(1, q)
+            complete_own(par, omega, q)
+
+        def odd(q):
+            @pl.when(more)
+            def _():
+                update_all(1, omega_odd, q)
+
+            start_sends(1 - par, 1, q, more)
+
+        own(0)
+        for q in range(chunks):
+            if q + 1 < chunks:
+                own(q + 1)
+            wait_arrivals(par, 1, q)
+            complete_halo(par, omega, q)
+            wait_sends(0, q)
+            update_all(0, omega_even, q, par)
+            start_sends(1 - par, 0, q, more)
+            if q > 0:
+                odd(q - 1)
+        odd(chunks - 1)
+        return carry
+
+    lax.fori_loop(0, rounds, round_body, 0)
+    for side in sides:
+        for has, copy in lone_copies(side, False):
+            @pl.when(has)
+            def _():
+                copy.wait_send()
     for q in range(chunks):
-        wait_sends(0, q)
-    for side in sides:
-        for q in range(chunks):
-            @pl.when(has_x[side])
-            def _():
-                edge_copy(side, q, 1 - side).wait_send()
-        for has, copy in side_copies(side, 1 - side):
+        for has, copy in raw_copies(q, False):
             @pl.when(has)
             def _():
                 copy.wait_send()
+
     for x in range(X):
         for b in range(blocks):
             start = (x * blocks + b) * Y
-            value = state[1, x, :, b * LANES : (b + 1) * LANES]
+            value = state[0, x, :, b * LANES : (b + 1) * LANES]
             flat[start : start + Y, :] = value
             out_ref[x, :, b * LANES : (b + 1) * LANES] = value
 
@@ -500,6 +549,21 @@
         row_copy(step).start()
 
     recv_rows[me] = send_rows[me]
+
+    @pl.loop(1, peers)
+    def _(step):
+        peer, place_of = peer_at(step)
+        pltpu.make_async_remote_copy(
+            send_slots.at[peer], recv_slots.at[peer], slot_send.at[peer], slot_recv.at[peer],
+            device_id=place_of, device_id_type=MESH).wait()
+
+    own = lax.broadcasted_iota(jnp.int32, (peers, CAP, LANES), 1)
+    lane_ids = lax.broadcasted_iota(jnp.int32, (peers, CAP, LANES), 2)
+    got = jnp.broadcast_to(recv_slots[...], (peers, CAP, LANES))
+    slot_of = jnp.sum(jnp.where(own == lane_ids, got, 0.0), axis=2, keepdims=True)
+    slot_of = slot_of.reshape(peers * CAP, 1)
+    slot_ids = lax.broadcasted_iota(jnp.int32, (peers * CAP, slots), 1).astype(jnp.float32)
+    chosen[...] = (slot_of == slot_ids).astype(jnp.float32).T.astype(jnp.bfloat16)
 
     @pl.loop(1, peers)
     def _(step):
@@ -564,8 +628,17 @@
             pltpu.VMEM((2, X, Z), f32),
             pltpu.VMEM((2, 2, 1, Z), f32),
             pltpu.VMEM((2, 2, 1, Z), f32),
-            pltpu.VMEM((2, 2, 1, Z), f32),
-            pltpu.VMEM((2, 2, 1, Z), f32),
+            pltpu.VMEM((2, Y, Z), f32),
+            pltpu.VMEM((2, X, Z), f32),
+            pltpu.VMEM((2, X, Z), f32),
+            pltpu.VMEM((2, 1, Z), f32),
+            pltpu.VMEM((2, 1, Z), f32),
+            pltpu.VMEM((2, 2, 2, 1, Z), f32),
+            pltpu.VMEM((2, 2, Y, Z), f32),
+            pltpu.VMEM((2, 2, X, Z), f32),
+            pltpu.VMEM((2, 1, Z), f32),
+            pltpu.VMEM((2, 1, Z), f32),
+            pltpu.VMEM((2, 2, 2, 1, Z), f32),
             pltpu.VMEM((X * Y * Z // LANES, LANES), f32),
             pltpu.VMEM((tiles, LANES), f32),
             pltpu.SMEM((tiles,), jnp.int32),
@@ -576,18 +649,16 @@
             pltpu.VMEM((peers, CAP, LANES), f32),
             pltpu.VMEM((peers, 1, LANES), f32),
             pltpu.VMEM((peers, 1, LANES), f32),
-            dma((2,)),
-            dma((2,)),
             dma((2, 2, chunks)),
             dma((2, 2, 2, chunks)),
             dma((2, 2, chunks)),
             dma((2, 2, 2, chunks)),
             dma((2, 2, chunks)),
             dma((2, 2, 2, chunks)),
-            dma((2, chunks)),
-            dma((2, chunks)),
-            dma((3, 2)),
-            dma((3, 2)),
+            dma((6, 2, chunks)),
+            dma((6, 2, chunks)),
+            dma((4, 2)),
+            dma((4, 2)),
             dma((peers,)),
             dma((peers,)),
             dma((peers,)),

time: 51.5 us -> 49.6 us (0.963)
  Pallas kernels: 50.7 us -> 48.8 us
    pallas_call x1, Pallas kernels: 49.5 us -> 47.6 us  [shards(): pl.pallas_call(functools.partial(kernel, n_x, n_y), out_shape=(pltpu.VMEM...]
where the time goes in v3:
time: 49.6 us; the launch traced here: 49.4 us
  Pallas kernels  48.8 us (98%)
  between operations  0.64 us (1%)
    pallas_call x1, Pallas kernels, shards(): pl.pallas_call(functools.partial(kernel, n_x, n_y), out_shape=(pltpu.VMEM...  47.6 us
    pallas_call x1, Pallas kernels, shards(): pl.pallas_call(hand_over, out_shape=tuple((jax.ShapeDtypeStruct(result.sh...  1.18 us

profile of v3, /device:TPU:0, one launch (start us, length us, event | category | flops | bytes accessed | tf_op | source)
XLA Modules:
  0.0 49.4 jit_solution(12198268377390114805)
XLA Ops:
  0.6 47.6 %shard_map.86 = (f32[8,32,1024]{2,1,0:T(8,128)S(1)}, f32[3,256,128]{2,1,0:T(8,128)S(1)}) custom-call(f32[8,32,1024]{2,1,0:T(8,128)} %grad_in.1, f32[3,8,32,1024]{3,2,1,0:T(8,128)} %beta_in.1, s32[256]{0:T(256)} %rows_in.1, s32[1,256]{1,0:T(1,128)} %bitcast.2, s32[1,256]{1,0:T(1,128)} %bitcast.3, s32[256,128]{1,0:T(8,128)} %mask_in.1, f32[3,256,128]{2,1,0:T(8,128)} %heights_in.1), custom_call_target="tpu_custom_call" | custom-call | tf_op jit(solution)/shard_map/pallas_call | solution.py:601
  48.2 1.2 %shard_map.87 = (f32[8,32,1024]{2,1,0:T(8,128)}, f32[3,256,128]{2,1,0:T(8,128)}) custom-call(f32[8,32,1024]{2,1,0:T(8,128)S(1)} %get-tuple-element.4.first_held, f32[3,256,128]{2,1,0:T(8,128)S(1)} %get-tuple-element.5.second_held), custom_call_target="tpu_custom_call" | custom-call | tf_op jit(solution)/shard_map/pallas_call | solution.py:672

commit v4 on v3

--- a/solution.py
+++ b/solution.py
@@ -77,22 +77,9 @@
     total = ITERS * STEPS
     rounds = (total - 2) // 2
 
-    for ref in (rim_x, rim_y, halo_x, halo_y, halo_d, edge_x, edge_y, line_x, line_y, raw_d):
-        ref[...] = jnp.zeros_like(ref)
-
-    def peer_at(step):
-        peer = (me + step) % peers
-        return peer, (peer // n_y, peer % n_y)
-
-    barrier = pltpu.get_barrier_semaphore()
-
-    @pl.loop(1, peers)
-    def _(step):
-        pl.semaphore_signal(barrier, inc=1, device_id=peer_at(step)[1], device_id_type=MESH)
-
-    names = ("owner", "slot", "beta", "grad", "rows", "mask", "heights")
+    names = ("beta", "grad", "owner", "slot", "rows", "mask", "heights")
     pairs = (
-        (owner_in, owner_ref), (slot_in, slot_ref), (beta_in, beta_ref), (grad_in, grad_ref),
+        (beta_in, beta_ref), (grad_in, grad_ref), (owner_in, owner_ref), (slot_in, slot_ref),
         (rows_in, rows_ref), (mask_in, mask_ref), (heights_in, heights_ref),
     )
     loads = {
@@ -101,27 +88,18 @@
     }
     for name in names:
         loads[name].start()
-    for name in ("owner", "slot"):
-        loads[name].wait()
-
-    owner = owner_ref[...]
-    peer_ids = lax.broadcasted_iota(jnp.int32, (peers, tiles), 0)
-    named = (owner == peer_ids).astype(jnp.float32)
-    down = lax.broadcasted_iota(jnp.int32, (tiles, tiles), 0)
-    across = lax.broadcasted_iota(jnp.int32, (tiles, tiles), 1)
-    earlier = (down < across).astype(jnp.bfloat16)
-    counts = jnp.dot(named.astype(jnp.bfloat16), earlier, preferred_element_type=jnp.float32)
-    position = jnp.sum(counts * named, axis=0, keepdims=True)
-    spot = owner.astype(jnp.float32) * CAP + position
-    spots = lax.broadcasted_iota(jnp.int32, (peers * CAP, tiles), 0).astype(jnp.float32)
-    place[...] = (spot == spots).astype(jnp.float32).astype(jnp.bfloat16)
-    spread = lax.broadcasted_iota(jnp.int32, (LANES, tiles), 0).astype(jnp.float32)
-    spread = (spread == position).astype(jnp.float32)
-    slot_rows = lax.dot_general(
-        named * slot_ref[...].astype(jnp.float32), spread, (((1,), (1,)), ((), ())),
-        preferred_element_type=jnp.float32, precision=EXACT,
-    )
-    send_slots[...] = slot_rows.reshape(peers, 1, LANES)
+    for ref in (rim_x, rim_y, halo_x, halo_y, halo_d, edge_x, edge_y, line_x, line_y, raw_d):
+        ref[...] = jnp.zeros_like(ref)
+
+    def peer_at(step):
+        peer = (me + step) % peers
+        return peer, (peer // n_y, peer % n_y)
+
+    barrier = pltpu.get_barrier_semaphore()
+
+    @pl.loop(1, peers, unroll=True)
+    def _(step):
+        pl.semaphore_signal(barrier, inc=1, device_id=peer_at(step)[1], device_id_type=MESH)
 
     z_ids = lax.broadcasted_iota(jnp.int32, (ROWS, Z), 1)
 
@@ -181,56 +159,95 @@
             send_rows.at[peer], recv_rows.at[me], row_send.at[peer], row_recv.at[me],
             device_id=place_of, device_id_type=MESH)
 
-    def lanes(q):
-        return pl.ds(q * WIDE, WIDE)
+    def reach(kind, q):
+        if kind == 0:
+            return q * WIDE, (q + 1) * WIDE
+        return max(q * WIDE - LANES, 0), ((q + 1) * WIDE - LANES if q < chunks - 1 else Z)
+
+    def lanes(q, kind=0):
+        start, stop = reach(kind, q)
+        return pl.ds(start, stop - start)
 
     def x_copy(par, kind, side, q, land):
         return remote(
-            state.at[kind, (X - 1) * side, :, lanes(q)], halo_x.at[par, kind, land, :, lanes(q)],
+            state.at[kind, (X - 1) * side, :, lanes(q, kind)], halo_x.at[par, kind, land, :, lanes(q, kind)],
             x_send.at[kind, side, q], x_recv.at[par, kind, land, q], at_x[side])
 
     def y_copy(par, kind, side, q, land):
         return remote(
-            face_y.at[kind, side, :, lanes(q)], halo_y.at[par, kind, land, :, lanes(q)],
-            y_send.at[kind, side, q], y_recv.at[par, kind, land, q], at_y[side])
+            face_y.at[kind, side, :, lanes(q, kind)], halo_y.at[par, kind, land, :, lanes(q, kind)],
+            y_send.at[kind, side, q], y_recv.at[par, kind, land, q], (ix, iy + 2 * side - 1))
 
     def d_copy(par, dx, dy, q, land):
         return remote(
             corner.at[dx, dy, :, lanes(q)], halo_d.at[par, land[0], land[1], :, lanes(q)],
             d_send.at[dx, dy, q], d_recv.at[par, land[0], land[1], q], (at_x[dx][0], at_y[dy][1]))
 
-    def copies_of(par, kind, q, arriving):
-        found = []
-        for side in sides:
-            land = side if arriving else 1 - side
-            found.append((has_x[side], x_copy(par, kind, side, q, land)))
-        for side in sides:
-            land = side if arriving else 1 - side
-            found.append((has_y[side], y_copy(par, kind, side, q, land)))
+    def each_side(act_x, act_y):
+        for side in sides:
+            @pl.when(has_x[side])
+            def _():
+                act_x(side)
+
+            @pl.when(has_y[side])
+            def _():
+                act_y(side)
+
+    def each_corner(act):
+        for dx in sides:
+            for dy in sides:
+                @pl.when(jnp.logical_and(has_x[dx], has_y[dy]))
+                def _():
+                    act(dx, dy)
+
+    def start_sends(par, kind, q):
+        for turn in sides:
+            side = (iy + turn) % 2
+
+            @pl.when(jnp.logical_and(iy + 2 * side - 1 >= 0, iy + 2 * side - 1 < n_y))
+            def _():
+                y_copy(par, kind, side, q, 1 - side).start()
+
         if kind == 0:
-            for dx in sides:
-                for dy in sides:
-                    land = (dx, dy) if arriving else (1 - dx, 1 - dy)
-                    found.append((jnp.logical_and(has_x[dx], has_y[dy]), d_copy(par, dx, dy, q, land)))
-        return found
-
-    def start_sends(par, kind, q, go=None):
-        for has, copy in copies_of(par, kind, q, False):
-            @pl.when(has if go is None else jnp.logical_and(has, go))
-            def _():
-                copy.start()
-
-    def wait_sends(kind, q):
-        for has, copy in copies_of(0, kind, q, False):
-            @pl.when(has)
-            def _():
-                copy.wait_send()
-
-    def wait_arrivals(par, kind, q):
-        for has, copy in copies_of(par, kind, q, True):
-            @pl.when(has)
-            def _():
-                copy.wait_recv()
+            each_corner(lambda dx, dy: d_copy(par, dx, dy, q, (1 - dx, 1 - dy)).start())
+        for side in sides:
+            @pl.when(has_x[side])
+            def _():
+                x_copy(par, kind, side, q, 1 - side).start()
+
+    def coming(q):
+        return [at for at in ((0, 1) if q == 0 else (q + 1,)) if at < chunks]
+
+    def wait_own(par, q):
+        def x_side(side):
+            x_copy(par, 0, side, q, side).wait_recv()
+            for at in coming(q):
+                x_copy(par, 1, side, at, 1 - side).wait_send()
+
+        def y_side(side):
+            y_copy(par, 0, side, q, side).wait_recv()
+            for at in coming(q):
+                y_copy(par, 1, side, at, 1 - side).wait_send()
+
+        def at_corner(dx, dy):
+            d_copy(par, dx, dy, q, (dx, dy)).wait_recv()
+            d_copy(par, dx, dy, q, (1 - dx, 1 - dy)).wait_send()
+
+        each_side(x_side, y_side)
+        each_corner(at_corner)
+
+    def wait_halo(par, q):
+        def x_side(side):
+            for at in coming(q):
+                x_copy(par, 1, side, at, side).wait_recv()
+            x_copy(par, 0, side, q, 1 - side).wait_send()
+
+        def y_side(side):
+            for at in coming(q):
+                y_copy(par, 1, side, at, side).wait_recv()
+            y_copy(par, 0, side, q, 1 - side).wait_send()
+
+        each_side(x_side, y_side)
 
     def lone_copies(side, arriving):
         land = side if arriving else 1 - side
@@ -335,43 +352,44 @@
         line_y[side, 0, :, cut] = raw_d[0, side, 0, :, cut] * inv[:1, :]
         line_y[side, 1, :, cut] = raw_bx[side, :, cut] * inv[X - 1 :, :]
 
-    def update(kind, omega, x, g, q, par=None):
+    def update_all(kind, omega, q, par=None):
         source = 1 - kind
-        r = slice(g * ROWS, (g + 1) * ROWS)
-        cut = slice(q * WIDE, (q + 1) * WIDE)
-        start, stop = max(q * WIDE - LANES, 0), min((q + 1) * WIDE + LANES, Z)
-        inner = slice(q * WIDE - start, q * WIDE - start + WIDE)
-        wide = state[source, x, r, start:stop]
-        s = wide[:, inner]
-        if g < groups - 1:
-            above_row = state[source, x, (g + 1) * ROWS : (g + 1) * ROWS + 1, cut]
-        else:
-            above_row = 0.0 if par is None else halo_y[par, 1, 1, x : x + 1, cut]
-        if g > 0:
-            below_row = state[source, x, g * ROWS - 1 : g * ROWS, cut]
-        else:
-            below_row = 0.0 if par is None else halo_y[par, 1, 0, x : x + 1, cut]
-        beside = target[x, r, cut] - s
-        beside += coeff[2, x, r, cut] * from_above(s, above_row)
-        beside += coeff[3, x, r, cut] * from_below(s, below_row)
-        beside += coeff[4, x, r, cut] * pltpu.roll(wide, stop - start - 1, 1)[:, inner]
-        beside += coeff[5, x, r, cut] * pltpu.roll(wide, 1, 1)[:, inner]
-        if x < X - 1:
-            beside += coeff[0, x, r, cut] * state[source, x + 1, r, cut]
-        elif par is not None:
-            beside += coeff[0, x, r, cut] * halo_x[par, 1, 1, r, cut]
-        if x > 0:
-            beside += coeff[1, x, r, cut] * state[source, x - 1, r, cut]
-        elif par is not None:
-            beside += coeff[1, x, r, cut] * halo_x[par, 1, 0, r, cut]
-        value = s + omega * beside
-        state[kind, x, r, cut] = value
-        keep_faces(kind, value, x, g, cut)
-
-    def update_all(kind, omega, q, par=None):
+        low, high = reach(kind, q)
+        cut = slice(low, high)
+        start, stop = max(low - LANES, 0), min(high + LANES, Z)
+        inner = slice(low - start, high - start)
+        rows = [slice(g * ROWS, (g + 1) * ROWS) for g in range(groups)]
+        at_top, at_bottom = row_index(high - low) == ROWS - 1, row_index(high - low) == 0
+
+        def plane(x):
+            return [state[source, x, r, start:stop] for r in rows]
+
+        before, here, after = None, plane(0), None
         for x in range(X):
-            for g in range(groups):
-                update(kind, omega, x, g, q, par)
+            after = plane(x + 1) if x < X - 1 else None
+            middle = [tile[:, inner] for tile in here]
+            ups = [pltpu.roll(tile, ROWS - 1, 0) for tile in middle]
+            downs = [pltpu.roll(tile, 1, 0) for tile in middle]
+            edges = [0.0, 0.0] if par is None else [halo_y[par, 1, side, x : x + 1, cut] for side in sides]
+            for g, r in enumerate(rows):
+                s = middle[g]
+                beside = target[x, r, cut] - s
+                beside += coeff[2, x, r, cut] * jnp.where(at_top, ups[g + 1] if g < groups - 1 else edges[1], ups[g])
+                beside += coeff[3, x, r, cut] * jnp.where(at_bottom, downs[g - 1] if g > 0 else edges[0], downs[g])
+                beside += coeff[4, x, r, cut] * pltpu.roll(here[g], stop - start - 1, 1)[:, inner]
+                beside += coeff[5, x, r, cut] * pltpu.roll(here[g], 1, 1)[:, inner]
+                if x < X - 1:
+                    beside += coeff[0, x, r, cut] * after[g][:, inner]
+                elif par is not None:
+                    beside += coeff[0, x, r, cut] * halo_x[par, 1, 1, r, cut]
+                if x > 0:
+                    beside += coeff[1, x, r, cut] * before[g]
+                elif par is not None:
+                    beside += coeff[1, x, r, cut] * halo_x[par, 1, 0, r, cut]
+                value = s + omega * beside
+                state[kind, x, r, cut] = value
+                keep_faces(kind, value, x, g, cut)
+            before, here = middle, after
 
     def complete_own(par, omega, q):
         cut = slice(q * WIDE, (q + 1) * WIDE)
@@ -387,7 +405,7 @@
                 state[1, x, row : row + 1, cut] += more[x : x + 1, :]
 
     def complete_halo(par, omega, q):
-        cut = slice(q * WIDE, (q + 1) * WIDE)
+        cut = slice(*reach(1, q))
         for side in sides:
             x = (X - 1) * side
             for g in range(groups):
@@ -415,7 +433,29 @@
             def _():
                 copy.start()
 
-    @pl.loop(1, peers)
+    for name in ("owner", "slot"):
+        loads[name].wait()
+
+    owner = owner_ref[...]
+    peer_ids = lax.broadcasted_iota(jnp.int32, (peers, tiles), 0)
+    named = (owner == peer_ids).astype(jnp.float32)
+    down = lax.broadcasted_iota(jnp.int32, (tiles, tiles), 0)
+    across = lax.broadcasted_iota(jnp.int32, (tiles, tiles), 1)
+    earlier = (down < across).astype(jnp.bfloat16)
+    counts = jnp.dot(named.astype(jnp.bfloat16), earlier, preferred_element_type=jnp.float32)
+    position = jnp.sum(counts * named, axis=0, keepdims=True)
+    spot = owner.astype(jnp.float32) * CAP + position
+    spots = lax.broadcasted_iota(jnp.int32, (peers * CAP, tiles), 0).astype(jnp.float32)
+    place[...] = (spot == spots).astype(jnp.float32).astype(jnp.bfloat16)
+    spread = lax.broadcasted_iota(jnp.int32, (LANES, tiles), 0).astype(jnp.float32)
+    spread = (spread == position).astype(jnp.float32)
+    slot_rows = lax.dot_general(
+        named * slot_ref[...].astype(jnp.float32), spread, (((1,), (1,)), ((), ())),
+        preferred_element_type=jnp.float32, precision=EXACT,
+    )
+    send_slots[...] = slot_rows.reshape(peers, 1, LANES)
+
+    @pl.loop(1, peers, unroll=True)
     def _(step):
         slot_copy(step).start()
 
@@ -479,9 +519,7 @@
             begin(q + 1)
         update_all(0, omega_of(STEPS - 1 - 1 % STEPS), q, 1)
         start_sends(0, 0, q)
-        if q > 0:
-            second(q - 1)
-    second(chunks - 1)
+        second(q)
 
     def round_body(number, carry):
         par = number % 2
@@ -491,29 +529,29 @@
         omega_odd = omega_at(2 * number + 4)
 
         def own(q):
-            wait_arrivals(par, 0, q)
-            wait_sends(1, q)
+            wait_own(par, q)
             complete_own(par, omega, q)
 
         def odd(q):
             @pl.when(more)
             def _():
                 update_all(1, omega_odd, q)
-
-            start_sends(1 - par, 1, q, more)
+                start_sends(1 - par, 1, q)
 
         own(0)
         for q in range(chunks):
             if q + 1 < chunks:
                 own(q + 1)
-            wait_arrivals(par, 1, q)
-            complete_halo(par, omega, q)
-            wait_sends(0, q)
+            wait_halo(par, q)
+            for at in coming(q):
+                complete_halo(par, omega, at)
             update_all(0, omega_even, q, par)
-            start_sends(1 - par, 0, q, more)
-            if q > 0:
-                odd(q - 1)
-        odd(chunks - 1)
+
+            @pl.when(more)
+            def _():
+                start_sends(1 - par, 0, q)
+
+            odd(q)
         return carry
 
     lax.fori_loop(0, rounds, round_body, 0)
@@ -544,13 +582,13 @@
     jumps = picked[...] * mask_ref[...].astype(jnp.float32)
     send_rows[...] = picked_sum(place[...], jumps).reshape(peers, CAP, LANES)
 
-    @pl.loop(1, peers)
+    @pl.loop(1, peers, unroll=True)
     def _(step):
         row_copy(step).start()
 
     recv_rows[me] = send_rows[me]
 
-    @pl.loop(1, peers)
+    @pl.loop(1, peers, unroll=True)
     def _(step):
         peer, place_of = peer_at(step)
         pltpu.make_async_remote_copy(
@@ -565,7 +603,7 @@
     slot_ids = lax.broadcasted_iota(jnp.int32, (peers * CAP, slots), 1).astype(jnp.float32)
     chosen[...] = (slot_of == slot_ids).astype(jnp.float32).T.astype(jnp.bfloat16)
 
-    @pl.loop(1, peers)
+    @pl.loop(1, peers, unroll=True)
     def _(step):
         peer, place_of = peer_at(step)
         pltpu.make_async_remote_copy(

time: 49.6 us -> 48.3 us (0.974)
  Pallas kernels: 48.8 us -> 47.5 us
    pallas_call x1, Pallas kernels: 47.6 us -> 46.3 us  [shards(): pl.pallas_call(functools.partial(kernel, n_x, n_y), out_shape=(pltpu.VMEM...]
where the time goes in v4:
time: 48.3 us; the launch traced here: 48.1 us
  Pallas kernels  47.5 us (98%)
  between operations  0.64 us (1%)
    pallas_call x1, Pallas kernels, shards(): pl.pallas_call(functools.partial(kernel, n_x, n_y), out_shape=(pltpu.VMEM...  46.3 us
    pallas_call x1, Pallas kernels, shards(): pl.pallas_call(hand_over, out_shape=tuple((jax.ShapeDtypeStruct(result.sh...  1.18 us

profile of v4, /device:TPU:0, one launch (start us, length us, event | category | flops | bytes accessed | tf_op | source)
XLA Modules:
  0.0 48.1 jit_solution(10642512756102300190)
XLA Ops:
  0.6 46.3 %shard_map.86 = (f32[8,32,1024]{2,1,0:T(8,128)S(1)}, f32[3,256,128]{2,1,0:T(8,128)S(1)}) custom-call(f32[8,32,1024]{2,1,0:T(8,128)} %grad_in.1, f32[3,8,32,1024]{3,2,1,0:T(8,128)} %beta_in.1, s32[256]{0:T(256)} %rows_in.1, s32[1,256]{1,0:T(1,128)} %bitcast.2, s32[1,256]{1,0:T(1,128)} %bitcast.3, s32[256,128]{1,0:T(8,128)} %mask_in.1, f32[3,256,128]{2,1,0:T(8,128)} %heights_in.1), custom_call_target="tpu_custom_call" | custom-call | tf_op jit(solution)/shard_map/pallas_call | solution.py:639
  46.9 1.2 %shard_map.87 = (f32[8,32,1024]{2,1,0:T(8,128)}, f32[3,256,128]{2,1,0:T(8,128)}) custom-call(f32[8,32,1024]{2,1,0:T(8,128)S(1)} %get-tuple-element.4.first_held, f32[3,256,128]{2,1,0:T(8,128)S(1)} %get-tuple-element.5.second_held), custom_call_target="tpu_custom_call" | custom-call | tf_op jit(solution)/shard_map/pallas_call | solution.py:710

commit v5 on v4

--- a/solution.py
+++ b/solution.py
@@ -201,6 +201,8 @@
                     act(dx, dy)
 
     def start_sends(par, kind, q):
+        if kind == 0:
+            each_corner(lambda dx, dy: d_copy(par, dx, dy, q, (1 - dx, 1 - dy)).start())
         for turn in sides:
             side = (iy + turn) % 2
 
@@ -208,8 +210,6 @@
             def _():
                 y_copy(par, kind, side, q, 1 - side).start()
 
-        if kind == 0:
-            each_corner(lambda dx, dy: d_copy(par, dx, dy, q, (1 - dx, 1 - dy)).start())
         for side in sides:
             @pl.when(has_x[side])
             def _():
@@ -555,23 +555,12 @@
         return carry
 
     lax.fori_loop(0, rounds, round_body, 0)
-    for side in sides:
-        for has, copy in lone_copies(side, False):
-            @pl.when(has)
-            def _():
-                copy.wait_send()
-    for q in range(chunks):
-        for has, copy in raw_copies(q, False):
-            @pl.when(has)
-            def _():
-                copy.wait_send()
-
+    keep = pltpu.make_async_copy(state.at[0], out_ref, load_sem.at[7])
+    keep.start()
     for x in range(X):
         for b in range(blocks):
             start = (x * blocks + b) * Y
-            value = state[0, x, :, b * LANES : (b + 1) * LANES]
-            flat[start : start + Y, :] = value
-            out_ref[x, :, b * LANES : (b + 1) * LANES] = value
+            flat[start : start + Y, :] = state[0, x, :, b * LANES : (b + 1) * LANES]
 
     @pl.loop(0, tiles // UNROLL)
     def _(part):
@@ -587,6 +576,16 @@
         row_copy(step).start()
 
     recv_rows[me] = send_rows[me]
+    for side in sides:
+        for has, copy in lone_copies(side, False):
+            @pl.when(has)
+            def _():
+                copy.wait_send()
+    for q in range(chunks):
+        for has, copy in raw_copies(q, False):
+            @pl.when(has)
+            def _():
+                copy.wait_send()
 
     @pl.loop(1, peers, unroll=True)
     def _(step):
@@ -613,6 +612,7 @@
     table = picked_sum(chosen[...], recv_rows[...].reshape(peers * CAP, LANES))
     for index in range(3):
         back_ref[index] = table * scales[index]
+    keep.wait()
 
 
 def hand_over(first_held, second_held, first_out, second_out, sem):

time: 48.3 us -> 47.9 us (level)
  no operation moved by 1% of the time
where the time goes in v5:
time: 47.9 us; the launch traced here: 47.8 us
  Pallas kernels  47.1 us (98%)
  between operations  0.64 us (1%)
    pallas_call x1, Pallas kernels, shards(): pl.pallas_call(functools.partial(kernel, n_x, n_y), out_shape=(pltpu.VMEM...  46 us
    pallas_call x1, Pallas kernels, shards(): pl.pallas_call(hand_over, out_shape=tuple((jax.ShapeDtypeStruct(result.sh...  1.18 us

profile of v5, /device:TPU:0, one launch (start us, length us, event | category | flops | bytes accessed | tf_op | source)
XLA Modules:
  0.0 47.8 jit_solution(9845911277479890522)
XLA Ops:
  0.6 46.0 %shard_map.86 = (f32[8,32,1024]{2,1,0:T(8,128)S(1)}, f32[3,256,128]{2,1,0:T(8,128)S(1)}) custom-call(f32[8,32,1024]{2,1,0:T(8,128)} %grad_in.1, f32[3,8,32,1024]{3,2,1,0:T(8,128)} %beta_in.1, s32[256]{0:T(256)} %rows_in.1, s32[1,256]{1,0:T(1,128)} %bitcast.2, s32[1,256]{1,0:T(1,128)} %bitcast.3, s32[256,128]{1,0:T(8,128)} %mask_in.1, f32[3,256,128]{2,1,0:T(8,128)} %heights_in.1), custom_call_target="tpu_custom_call" | custom-call | tf_op jit(solution)/shard_map/pallas_call | solution.py:639
  46.6 1.2 %shard_map.87 = (f32[8,32,1024]{2,1,0:T(8,128)}, f32[3,256,128]{2,1,0:T(8,128)}) custom-call(f32[8,32,1024]{2,1,0:T(8,128)S(1)} %get-tuple-element.4.first_held, f32[3,256,128]{2,1,0:T(8,128)S(1)} %get-tuple-element.5.second_held), custom_call_target="tpu_custom_call" | custom-call | tf_op jit(solution)/shard_map/pallas_call | solution.py:710
